TPU v7x, 32 devices: a whole 2x2x4 slice. The times are simulated.
32 devices in a mesh: stream: 4 (over x, core), cross: 8 (over z, y).
Axes of the slice: x: 2, y: 2, z: 4, core: 2. Of those that a mesh axis runs over, the one named last changes fastest.
Arguments:
- state_now: float32 [7, 8, 64, 512], P(None, None, 'cross', 'stream'), as said below
- state_base: float32 [7, 8, 64, 512], P(None, None, 'cross', 'stream'), as said below
- inflow: float32 [7, 8, 64, 3], P(None, None, 'cross'), as said below
Outputs:
- state_next: float32 [7, 8, 64, 512], P(None, None, 'cross', 'stream')
Inputs may be any that keep to these rules, and one draw needn't show every extreme that they name: `state_now`: partial densities and volume fractions are positive, volume fractions below 1, and the pressure that each cell implies is positive. `state_base`: partial densities and volume fractions are positive, volume fractions below 1, and the pressure that each cell implies is positive. `inflow`: partial densities and volume fractions are positive, volume fractions below 1, and the pressure that each cell implies is positive.
All inputs are finite; a program needn't handle non-finite values.
Results may differ from a plain program's by a relative error of at most 0.0003.
Values sent between devices are 32-bit elements; how exact they have to be, the bound alone decides.
No kernel may reach another device: no remote copies, remote signals or barrier semaphores. Data moves between devices by JAX's collectives and lax.ppermute only.
A program may use at most 64 MiB of HBM per device.

v0:
```python
import jax
import jax.numpy as jnp
from jax import lax
from jax.sharding import PartitionSpec as P

gas_gamma = 1.4
liquid_gamma = 4.4
liquid_stiff = 0.6
courant = 0.3
weno_epsilon = 1e-06


def with_halo(array, sides, width, wrap):
    for axis, dim in sides:
        size, length = (lax.axis_size(axis), array.shape[dim])
        up = [(i, (i + 1) % size) for i in range(size if wrap else size - 1)]
        down = [(j, i) for i, j in up]
        last = lax.slice_in_dim(array, length - width, length, axis=dim)
        first = lax.slice_in_dim(array, 0, width, axis=dim)
        before = lax.ppermute(last, axis, up)
        after = lax.ppermute(first, axis, down)
        array = jnp.concatenate([before, array, after], axis=dim)
    return array


def mixture(volume):
    stiff_gamma = volume / (gas_gamma - 1.0) + (1.0 - volume) / (liquid_gamma - 1.0)
    stiff_term = (1.0 - volume) * liquid_gamma * liquid_stiff / (liquid_gamma - 1.0)
    return (stiff_gamma, stiff_term)


def primitive(conserved):
    density = conserved[0] + conserved[1]
    vel_one = conserved[2] / density
    vel_two = conserved[3] / density
    vel_three = conserved[4] / density
    kinetic = 0.5 * (conserved[2] * vel_one + conserved[3] * vel_two + conserved[4] * vel_three)
    stiff_gamma, stiff_term = mixture(conserved[6])
    pressure = (conserved[5] - kinetic - stiff_term) / stiff_gamma
    return jnp.stack(
        [conserved[0], conserved[1], vel_one, vel_two, vel_three, pressure, conserved[6]]
    )


def sound(primitives):
    density = primitives[0] + primitives[1]
    stiff_gamma, stiff_term = mixture(primitives[6])
    return jnp.sqrt(((stiff_gamma + 1.0) * primitives[5] + stiff_term) / (stiff_gamma * density))


def max_speed(conserved):
    primitives = primitive(conserved)
    fastest = jnp.maximum(
        jnp.maximum(jnp.abs(primitives[2]), jnp.abs(primitives[3])), jnp.abs(primitives[4])
    )
    return jnp.max(fastest + sound(primitives))


def weno_face(far_left, near_left, centre, near_right, far_right):
    first_low = far_left - 2.0 * near_left + centre
    second_low = far_left - 4.0 * near_left + 3.0 * centre
    first_mid = near_left - 2.0 * centre + near_right
    second_mid = near_left - near_right
    first_high = centre - 2.0 * near_right + far_right
    second_high = 3.0 * centre - 4.0 * near_right + far_right
    smooth_low = weno_epsilon + 13.0 / 12.0 * first_low * first_low + 0.25 * second_low * second_low
    smooth_mid = weno_epsilon + 13.0 / 12.0 * first_mid * first_mid + 0.25 * second_mid * second_mid
    smooth_high = (
        weno_epsilon + 13.0 / 12.0 * first_high * first_high + 0.25 * second_high * second_high
    )
    weight_low = 0.1 / (smooth_low * smooth_low)
    weight_mid = 0.6 / (smooth_mid * smooth_mid)
    weight_high = 0.3 / (smooth_high * smooth_high)
    guess_low = (2.0 * far_left - 7.0 * near_left + 11.0 * centre) / 6.0
    guess_mid = (-near_left + 5.0 * centre + 2.0 * near_right) / 6.0
    guess_high = (2.0 * centre + 5.0 * near_right - far_right) / 6.0
    return (weight_low * guess_low + weight_mid * guess_mid + weight_high * guess_high) / (
        weight_low + weight_mid + weight_high
    )


def clamp_face(state, lower_cell, upper_cell):
    smaller = jnp.minimum(lower_cell, upper_cell)
    larger = jnp.maximum(lower_cell, upper_cell)
    limited = []
    for component in range(7):
        face_value = state[component]
        if component in (0, 1, 5):
            face_value = jnp.maximum(face_value, 0.5 * smaller[component])
        elif component == 6:
            face_value = jnp.clip(face_value, 0.5 * smaller[6], 1.0 - 0.5 * (1.0 - larger[6]))
        limited.append(face_value)
    return jnp.stack(limited)


def side_terms(primitives, normal):
    density = primitives[0] + primitives[1]
    stiff_gamma, stiff_term = mixture(primitives[6])
    velocity = [primitives[2], primitives[3], primitives[4]]
    energy = (
        stiff_gamma * primitives[5]
        + stiff_term
        + 0.5
        * density
        * (velocity[0] * velocity[0] + velocity[1] * velocity[1] + velocity[2] * velocity[2])
    )
    normal_vel = velocity[normal]
    amounts = jnp.stack(
        [
            primitives[0],
            primitives[1],
            density * velocity[0],
            density * velocity[1],
            density * velocity[2],
            energy,
            primitives[6],
        ]
    )
    momentum = []
    for component in range(3):
        moved = density * velocity[component] * normal_vel
        if component == normal:
            moved = moved + primitives[5]
        momentum.append(moved)
    transport = jnp.stack(
        [
            primitives[0] * normal_vel,
            primitives[1] * normal_vel,
            momentum[0],
            momentum[1],
            momentum[2],
            (energy + primitives[5]) * normal_vel,
            primitives[6] * normal_vel,
        ]
    )
    signal = jnp.abs(normal_vel) + sound(primitives)
    return (amounts, transport, normal_vel, signal)


def face_flux(left_state, right_state, normal):
    amount_left, transport_left, normal_left, signal_left = side_terms(left_state, normal)
    amount_right, transport_right, normal_right, signal_right = side_terms(right_state, normal)
    fastest = jnp.maximum(signal_left, signal_right)
    face_fluxes = 0.5 * (transport_left + transport_right) - 0.5 * fastest * (
        amount_right - amount_left
    )
    return (face_fluxes, 0.5 * (normal_left + normal_right))


def direction_sweep(padded, dimension, normal):
    primitives = primitive(padded)
    length = padded.shape[dimension] - 6
    pieces = [
        lax.slice_in_dim(primitives, offset, offset + length + 1, axis=dimension)
        for offset in range(6)
    ]
    left_state = clamp_face(
        weno_face(pieces[0], pieces[1], pieces[2], pieces[3], pieces[4]), pieces[2], pieces[3]
    )
    right_state = clamp_face(
        weno_face(pieces[5], pieces[4], pieces[3], pieces[2], pieces[1]), pieces[2], pieces[3]
    )
    face_fluxes, face_motion = face_flux(left_state, right_state, normal)
    change = lax.slice_in_dim(face_fluxes, 1, length + 1, axis=dimension) - lax.slice_in_dim(
        face_fluxes, 0, length, axis=dimension
    )
    spread = lax.slice_in_dim(face_motion, 1, length + 1, axis=dimension - 1) - lax.slice_in_dim(
        face_motion, 0, length, axis=dimension - 1
    )
    return (change, spread)


def tendency(stream_cells, cross_cells, span_cells, centre_cells):
    change_stream, spread_stream = direction_sweep(stream_cells, 3, 0)
    change_cross, spread_cross = direction_sweep(cross_cells, 2, 1)
    change_span, spread_span = direction_sweep(span_cells, 1, 2)
    total = -(change_stream + change_cross + change_span)
    source = centre_cells[6] * (spread_stream + spread_cross + spread_span)
    return jnp.concatenate([total[:6], (total[6] + source)[None]], axis=0)


def shards(state_now, state_base, inflow):
    fastest_here = max_speed(state_base)
    slab_fastest = lax.pmax(fastest_here, "cross")
    fastest = lax.pmax(slab_fastest, "stream")
    time_step = courant / fastest
    cross_cells = with_halo(state_now, (("cross", 2),), 3, True)
    stream_cells = with_halo(state_now, (("stream", 3),), 3, False)
    position = lax.axis_index("stream")
    final_index = lax.axis_size("stream") - 1
    last_cells = jnp.repeat(state_now[:, :, :, -1:], 3, axis=3)
    lower_rim = jnp.where(position == 0, inflow, stream_cells[:, :, :, :3])
    upper_rim = jnp.where(position == final_index, last_cells, stream_cells[:, :, :, -3:])
    stream_cells = jnp.concatenate([lower_rim, state_now, upper_rim], axis=3)
    span_cells = jnp.concatenate([state_now[:, -3:], state_now, state_now[:, :3]], axis=1)
    changes = tendency(stream_cells, cross_cells, span_cells, state_now)
    return state_base / 3.0 + 2.0 / 3.0 * (state_now + time_step * changes)


def solution(mesh):
    return jax.shard_map(
        shards,
        mesh=mesh,
        in_specs=(
            P(None, None, "cross", "stream"),
            P(None, None, "cross", "stream"),
            P(None, None, "cross", None),
        ),
        out_specs=P(None, None, "cross", "stream"),
        check_vma=False,
    )
```

profile of v0, /device:TPU:0, one launch (start us, length us, event | category | flops | bytes accessed | tf_op | source)
XLA Modules:
  0.0 58.4 jit_solution(12315351350939984382)
XLA Ops:
  0.0 1.0 %copy.21 = f32[7,8,8,128]{3,1,2,0:T(8,128)S(1)} copy(f32[7,8,8,128]{3,2,1,0:T(8,128)} %param.3) | data formatting | bytes 458752 | tf_op args[0]
  1.0 0.8 %fusion.162 = (f32[7,8,8,3]{3,1,2,0:T(8,128)}, f32[7,8,8,3]{3,1,2,0:T(8,128)}) fusion(f32[7,8,8,128]{3,1,2,0:T(8,128)S(1)} %copy.21), kind=kLoop, calls=%fused_computation.423 | loop fusion | bytes 21504 | tf_op jit(solution)/shard_map/slice | solution.py:18
  1.8 1.3 %collective-permute-start.1 = (f32[7,8,8,3]{3,1,2,0:T(8,128)}, f32[7,8,8,3]{3,1,2,0:T(8,128)}, u32[]{:S(2)}, u32[]{:S(2)}) collective-permute-start(f32[7,8,8,3]{3,1,2,0:T(8,128)} %get-tuple-element.129), channel_id=1, source_target_pairs={{8,0},{16,8},{24,16},{9,1},{17,9},{25,17},{10,2},{18,10},{26,18},{... | collective-permute-start | bytes 16136 | tf_op jit(solution)/shard_map/ppermute | solution.py:21
  3.1 3.7 %collective-permute-start = (f32[7,8,8,3]{3,1,2,0:T(8,128)}, f32[7,8,8,3]{3,1,2,0:T(8,128)}, u32[]{:S(2)}, u32[]{:S(2)}) collective-permute-start(f32[7,8,8,3]{3,1,2,0:T(8,128)} %get-tuple-element.128), channel_id=1, source_target_pairs={{0,8},{8,16},{16,24},{1,9},{9,17},{17,25},{2,10},{10,18},{18,26},{... | collective-permute-start | bytes 16136 | tf_op jit(solution)/shard_map/ppermute | solution.py:20
  6.8 0.7 %fusion.163 = (f32[7,8,3,128]{3,1,2,0:T(8,128)}, f32[7,8,3,128]{3,1,2,0:T(8,128)}) fusion(f32[7,8,8,128]{3,1,2,0:T(8,128)S(1)} %copy.21), kind=kLoop, calls=%fused_computation.424 | loop fusion | bytes 344064 | tf_op jit(solution)/shard_map/slice | solution.py:19
  7.5 3.0 %collective-permute-start.2 = (f32[7,8,3,128]{3,1,2,0:T(8,128)}, f32[7,8,3,128]{3,1,2,0:T(8,128)}, u32[]{:S(2)}, u32[]{:S(2)}) collective-permute-start(f32[7,8,3,128]{3,1,2,0:T(8,128)} %get-tuple-element.131), channel_id=1, source_target_pairs={{0,1},{1,2},{2,3},{3,4},{4,5},{5,6},{6,7},{7,0},{8,9},{9,10},{10,1... | collective-permute-start | bytes 258056 | tf_op jit(solution)/shard_map/ppermute | solution.py:20
  10.5 3.0 %collective-permute-start.3 = (f32[7,8,3,128]{3,1,2,0:T(8,128)}, f32[7,8,3,128]{3,1,2,0:T(8,128)}, u32[]{:S(2)}, u32[]{:S(2)}) collective-permute-start(f32[7,8,3,128]{3,1,2,0:T(8,128)} %get-tuple-element.130), channel_id=1, source_target_pairs={{1,0},{2,1},{3,2},{4,3},{5,4},{6,5},{7,6},{0,7},{9,8},{10,9},{11,1... | collective-permute-start | bytes 258056 | tf_op jit(solution)/shard_map/ppermute | solution.py:21
  13.9 2.1 %fusion.160 = (f32[7,9,8,128]{3,1,2,0:T(8,128)S(1)}, f32[7,9,8,128]{3,1,2,0:T(8,128)S(1)}, f32[7,9,8,128]{3,1,2,0:T(8,128)S(1)}, f32[7,9,8,128]{3,1,2,0:T(8,128)S(1)}, f32[7,9,8,128]{3,1,2,0:T(8,128)S(1)}) fusion(f32[7,14,8,128]{3,1,2,0:T(8,128)S(1)} %constant_dynamic-update-slice_fusion.71), kind=kLoop, calls=%fused_computation.421 | loop fusion | flops 8064000 | bytes 2838528 | tf_op jit(solution)/shard_map/slice | solution.py:154
  16.0 0.8 %multiply_bitcast_fusion.1 = (f32[9,8,128]{2,0,1:T(8,128)}, f32[1,9,8,128]{3,1,2,0:T(8,128)S(1)}, f32[1,9,8,128]{3,1,2,0:T(8,128)S(1)}, f32[1,9,8,128]{3,1,2,0:T...) fusion(f32[7,9,8,128]{3,1,2,0:T(8,128)S(1)} %get-tuple-element., ...), kind=kLoop, calls=%fused_computation.322 | loop fusion | flops 433151 | bytes 1085440 | tf_op jit(solution)/shard_map/mul | solution.py:144
  17.0 0.5 copy-done.2
  17.4 0.9 %copy-done.1 = f32[7,8,8,128]{3,2,1,0:T(8,128)S(1)} copy-done((f32[7,8,8,128]{3,2,1,0:T(8,128)S(1)}, f32[7,8,8,128]{3,2,1,0:T(8,128)}, u32[]{:S(2)}) %copy-start.1) | copy-done | bytes 229400
  18.3 0.7 %add_reduce_fusion = f32[]{:T(128)} fusion(f32[7,8,8,128]{3,2,1,0:T(8,128)S(1)} %copy-done.1), kind=kLoop, calls=%fused_computation.409 | loop fusion | flops 245759 | bytes 229380 | tf_op jit(solution)/shard_map/reduce_max | solution.py:56
  19.1 19.7 %pmax.14 = f32[]{:T(128)} all-reduce(f32[]{:T(128)} %add_reduce_fusion), channel_id=1, replica_groups=mesh['stream'=4,'cross'=8] {'cross'}, use_global_device_ids=true, to_apply=%region_1.0 | all-reduce | flops 1 | bytes 8 | tf_op jit(solution)/shard_map/pmax | solution.py:184
  38.9 0.9 %constant_dynamic-update-slice_fusion.78 = (f32[7,9,8,128]{3,1,2,0:T(8,128)S(1)}, f32[1,9,8,128]{3,1,2,0:T(8,128)S(1)}, f32[7,9,8,128]{3,1,2,0:T(8,128)S(1)}, f3...) fusion(f32[7,9,8,128]{3,1,2,0:T(8,128)S(1)} %get-tuple-element.65, ...), kind=kLoop, calls=%fused_computation.247 | loop fusion | flops 331776 | bytes 1150976
  39.9 0.8 %copy-done.3 = f32[9,8,128]{2,0,1:T(8,128)S(1)} copy-done((f32[9,8,128]{2,0,1:T(8,128)S(1)}, f32[9,8,128]{2,0,1:T(8,128)}, u32[]{:S(2)}) %copy-start.3) | copy-done | bytes 36888
  40.8 6.3 %pmax.15 = f32[]{:T(128)} all-reduce(f32[]{:T(128)} %pmax.14), channel_id=1, replica_groups=mesh['stream'=4,'cross'=8] {'stream'}, use_global_device_ids=true, to_apply=%region_2.0 | all-reduce | flops 1 | bytes 8 | tf_op jit(solution)/shard_map/pmax | solution.py:185
  47.2 0.4 copy.24
  47.6 0.5 copy-done.4
  49.2 1.1 %broadcast_select_fusion = f32[7,8,8,3]{3,1,2,0:T(8,128)S(1)} fusion(f32[7,8,8,3]{3,1,2,0:T(8,128)} %collective-permute-done.1, f32[7,8,8]{1,2,0:T(8,128)S(1)} %bitcast.107, pred[]{:T(512)S(6)} %eq.7), kind=kLoop, calls=%fused_computation.274 | loop fusion | flops 1344 | bytes 12545 | tf_op jit(solution)/shard_map/jit(_where)/select_n | solution.py:193
  50.8 2.2 %fusion.159 = (f32[7,8,8,129]{3,1,2,0:T(8,128)S(1)}, f32[7,8,8,129]{3,1,2,0:T(8,128)S(1)}, f32[7,8,8,129]{3,1,2,0:T(8,128)S(1)}, f32[7,8,8,129]{3,1,2,0:T(8,128)S(1)}, f32[7,8,8,129]{3,1,2,0:T(8,128)S(1)}) fusion(f32[7,8,8,134]{3,1,2,0:T(8,128)S(1)} %constant_dynamic-update-slice_fusion), kind=kLoop, calls=%fused_computation.420 | loop fusion | flops 7224000 | bytes 2542848 | tf_op jit(solution)/shard_map/slice | solution.py:154
  53.7 0.9 %constant_dynamic-update-slice_fusion.36 = f32[7,8,14,128]{3,1,2,0:T(8,128)S(1)} fusion(f32[7,8,3,128]{3,1,2,0:T(8,128)} %collective-permute-done.2), kind=kLoop, calls=%fused_computation.205 | loop fusion | bytes 172032
  54.6 0.9 %constant_dynamic-update-slice_fusion.34 = f32[7,8,14,128]{3,1,2,0:T(8,128)S(1)} fusion(f32[7,8,14,128]{3,1,2,0:T(8,128)S(1)} %constant_dynamic-update-slice_fusion.35, f32[7,8,3,128]{3,1,2,0:T(8,128)} %collective-permute-done.3), kind=kLoop, calls=%fused_computation.203 | loop fusion | bytes 172032 | tf_op jit(solution)/shard_map/concatenate | solution.py:22
  55.7 1.1 %fusion.161 = (f32[7,8,9,128]{3,1,2,0:T(8,128)S(1)}, f32[7,8,9,128]{3,1,2,0:T(8,128)S(1)}, f32[7,8,9,128]{3,1,2,0:T(8,128)S(1)}, f32[7,8,9,128]{3,1,2,0:T(8,128)S(1)}, f32[7,8,9,128]{3,1,2,0:T(8,128)S(1)}) fusion(f32[7,8,14,128]{3,1,2,0:T(8,128)S(1)} %constant_dynamic-update-slice_fusion.37), kind=kLoop, calls=%fused_computation.422 | loop fusion | flops 8064000 | bytes 2838528 | tf_op jit(solution)/shard_map/slice | solution.py:154
  57.7 0.7 %copy.22 = f32[7,8,8,128]{3,2,1,0:T(8,128)} copy(f32[7,8,8,128]{3,1,2,0:T(8,128)S(1)} %fusion.107) | data formatting | bytes 458752 | tf_op jit(solution)/shard_map/add | solution.py:197
  (80 shorter events, 3.1 us)
Async XLA Ops:
  1.8 47.4 %collective-permute-start.1 = (f32[7,8,8,3]{3,1,2,0:T(8,128)}, f32[7,8,8,3]{3,1,2,0:T(8,128)}, u32[]{:S(2)}, u32[]{:S(2)}) collective-permute-start(f32[7,8,8,3]{3,1,2,0:T(8,128)} %get-tuple-element.129), channel_id=1, source_target_pairs={{8,0},{16,8},{24,16},{9,1},{17,9},{25,17},{10,2},{18,10},{26,18},{... | collective-permute-start | bytes 16136 | tf_op jit(solution)/shard_map/ppermute | solution.py:21
  3.1 47.2 %collective-permute-start = (f32[7,8,8,3]{3,1,2,0:T(8,128)}, f32[7,8,8,3]{3,1,2,0:T(8,128)}, u32[]{:S(2)}, u32[]{:S(2)}) collective-permute-start(f32[7,8,8,3]{3,1,2,0:T(8,128)} %get-tuple-element.128), channel_id=1, source_target_pairs={{0,8},{8,16},{16,24},{1,9},{9,17},{17,25},{2,10},{10,18},{18,26},{... | collective-permute-start | bytes 16136 | tf_op jit(solution)/shard_map/ppermute | solution.py:20
  7.5 46.1 %collective-permute-start.2 = (f32[7,8,3,128]{3,1,2,0:T(8,128)}, f32[7,8,3,128]{3,1,2,0:T(8,128)}, u32[]{:S(2)}, u32[]{:S(2)}) collective-permute-start(f32[7,8,3,128]{3,1,2,0:T(8,128)} %get-tuple-element.131), channel_id=1, source_target_pairs={{0,1},{1,2},{2,3},{3,4},{4,5},{5,6},{6,7},{7,0},{8,9},{9,10},{10,1... | collective-permute-start | bytes 258056 | tf_op jit(solution)/shard_map/ppermute | solution.py:20
  10.5 44.1 %collective-permute-start.3 = (f32[7,8,3,128]{3,1,2,0:T(8,128)}, f32[7,8,3,128]{3,1,2,0:T(8,128)}, u32[]{:S(2)}, u32[]{:S(2)}) collective-permute-start(f32[7,8,3,128]{3,1,2,0:T(8,128)} %get-tuple-element.130), channel_id=1, source_target_pairs={{1,0},{2,1},{3,2},{4,3},{5,4},{6,5},{7,6},{0,7},{9,8},{10,9},{11,1... | collective-permute-start | bytes 258056 | tf_op jit(solution)/shard_map/ppermute | solution.py:21
  16.8 0.6 %copy-start.2 = (f32[1,9,8,128]{3,1,2,0:T(8,128)}, f32[1,9,8,128]{3,1,2,0:T(8,128)S(1)}, u32[]{:S(2)}) copy-start(f32[1,9,8,128]{3,1,2,0:T(8,128)S(1)} %get-tuple-element.32) | copy-start | bytes 110596
  17.4 0.9 %copy-start.1 = (f32[7,8,8,128]{3,2,1,0:T(8,128)S(1)}, f32[7,8,8,128]{3,2,1,0:T(8,128)}, u32[]{:S(2)}) copy-start(f32[7,8,8,128]{3,2,1,0:T(8,128)} %param.4) | copy-start | bytes 688132
  39.8 0.8 %copy-start.3 = (f32[9,8,128]{2,0,1:T(8,128)S(1)}, f32[9,8,128]{2,0,1:T(8,128)}, u32[]{:S(2)}) copy-start(f32[9,8,128]{2,0,1:T(8,128)} %get-tuple-element.27) | copy-start | bytes 110596
  40.7 6.4 %copy-start = (f32[7,8,8,128]{3,2,1,0:T(8,128)S(1)}, f32[7,8,8,128]{3,2,1,0:T(8,128)}, u32[]{:S(2)}) copy-start(f32[7,8,8,128]{3,2,1,0:T(8,128)} %param.3) | copy-start | bytes 688132
  47.2 0.9 %copy-start.4 = (f32[7,8,8,3]{2,1,3,0:T(8,128)S(1)}, f32[7,8,8,3]{2,1,3,0:T(8,128)}, u32[]{:S(2)}) copy-start(f32[7,8,8,3]{2,1,3,0:T(8,128)} %param.5) | copy-start | bytes 16132
where the time goes:
time: 59.2 us; the launch traced here: 58.4 us
  blocking collectives  26 us (44%)
  other arithmetic  11.3 us (19%)
  starting transfers between devices  11.1 us (19%)
  local copies, waits for them, and re-layouts  8.78 us (15%)
  between operations  1.22 us (2%)
    pmax x1, blocking collectives, shards(): slab_fastest = lax.pmax(fastest_here, 'cross')  19.7 us
    ppermute x2, starting transfers between devices, with_halo(): before = lax.ppermute(last, axis, up)  6.74 us
    pmax x1, blocking collectives, shards(): fastest = lax.pmax(slab_fastest, 'stream')  6.25 us
    slice x3, other arithmetic, direction_sweep(): lax.slice_in_dim(primitives, offset, offset + length + 1, axis=dimension)  5.44 us
    unnamed x23, local copies, waits for them, and re-layouts  5.02 us
    ppermute x2, starting transfers between devices, with_halo(): after = lax.ppermute(first, axis, down)  4.32 us
    unnamed x38, other arithmetic  1.91 us
  transfers between devices with their start and end apart: 4, of which 0 were waited for; matrix products, arithmetic and copies ran while one was open for 21% of the time, Pallas kernels for 0%

commit v1 on v0

v1 whole, which is shorter than its diff:
```python
import functools

import jax
import jax.numpy as jnp
from jax import lax
from jax.experimental import pallas as pl
from jax.experimental.pallas import tpu as pltpu
from jax.sharding import PartitionSpec as P

gas_gamma = 1.4
liquid_gamma = 4.4
liquid_stiff = 0.6
courant = 0.3
weno_epsilon = 1e-06
ghost = 3
fields = 7


def reciprocal(value):
    guess = pl.reciprocal(value, approx=True)
    return guess * (2.0 - value * guess)


def mixture(volume):
    rest = 1.0 - volume
    stiff_gamma = volume * (1.0 / (gas_gamma - 1.0)) + rest * (1.0 / (liquid_gamma - 1.0))
    stiff_term = rest * (liquid_gamma * liquid_stiff / (liquid_gamma - 1.0))
    return stiff_gamma, stiff_term


def primitive(u):
    inverse = reciprocal(u[0] + u[1])
    v = [u[2] * inverse, u[3] * inverse, u[4] * inverse]
    kinetic = 0.5 * (u[2] * v[0] + u[3] * v[1] + u[4] * v[2])
    stiff_gamma, stiff_term = mixture(u[6])
    pressure = (u[5] - kinetic - stiff_term) * reciprocal(stiff_gamma)
    return [u[0], u[1], v[0], v[1], v[2], pressure, u[6]]


def sound(w, density, stiff_gamma, stiff_term):
    top = (stiff_gamma + 1.0) * w[5] + stiff_term
    return jnp.sqrt(top * reciprocal(stiff_gamma * density))


def weno_cell(a, b, c, d, h):
    low, mid, high = b - a, c - b, d - c
    e_low, e_mid, e_high = 3.0 * b - a, b + c, d - 3.0 * c

    def weight(bend, slope):
        smooth = weno_epsilon + (13.0 / 12.0) * (bend * bend) + 0.25 * (slope * slope)
        r = reciprocal(jnp.minimum(smooth, 1e38))
        return r * r

    w_low, w_mid, w_high = weight(low, e_low), 6.0 * weight(mid, e_mid), weight(high, e_high)
    low3, high3 = 3.0 * w_low, 3.0 * w_high
    total_up = (w_low + high3) + w_mid
    total_down = (low3 + w_high) + w_mid
    up = w_low * (5.0 * b - 2.0 * a) + w_mid * (b + 2.0 * c) + high3 * (4.0 * c - d)
    down = w_high * (5.0 * c - 2.0 * d) + w_mid * (c + 2.0 * b) + low3 * (4.0 * b - a)
    up = h + up * (reciprocal(total_up) * (1.0 / 6.0))
    down = h - down * (reciprocal(total_down) * (1.0 / 6.0))
    return up, down


def limit(component, value, first, second):
    if component in (0, 1, 5):
        return jnp.maximum(value, 0.5 * jnp.minimum(first, second))
    if component == 6:
        smaller = 0.5 * jnp.minimum(first, second)
        larger = 1.0 - 0.5 * (1.0 - jnp.maximum(first, second))
        return jnp.minimum(jnp.maximum(value, smaller), larger)
    return value


def cell_faces(component, a, b, c, d, h):
    up, down = weno_cell(a, b, c, d, h)
    return limit(component, up, h, h + c), limit(component, down, h - b, h)


def side_terms(w, normal):
    density = w[0] + w[1]
    stiff_gamma, stiff_term = mixture(w[6])
    v = w[2:5]
    mom = [density * x for x in v]
    energy = stiff_gamma * w[5] + stiff_term + 0.5 * (mom[0] * v[0] + mom[1] * v[1] + mom[2] * v[2])
    vn = v[normal]
    amounts = [w[0], w[1], mom[0], mom[1], mom[2], energy, w[6]]
    moved = [x * vn for x in amounts]
    moved[2 + normal] = moved[2 + normal] + w[5]
    moved[5] = moved[5] + w[5] * vn
    return amounts, moved, vn, jnp.abs(vn) + sound(w, density, stiff_gamma, stiff_term)


def face_flux(left, right, normal):
    ul, fl, vl, sl = side_terms(left, normal)
    ur, fr, vr, sr = side_terms(right, normal)
    half = 0.5 * jnp.maximum(sl, sr)
    flux = [0.5 * (fl[i] + fr[i]) - half * (ur[i] - ul[i]) for i in range(fields)]
    return flux + [0.5 * (vl + vr)]


def lane_of(shape):
    return lax.broadcasted_iota(jnp.int32, shape, 1)


def pack_kernel(now_ref, base_ref, inflow_ref, w_ref, up_ref, down_ref, edge_ref, in_ref):
    nz, ny, nx = now_ref.shape[1:]
    seg = nx // ny
    lane = lane_of((nz, nx))

    edge_ref[...] = jnp.zeros(edge_ref.shape, jnp.float32)
    fastest = None
    for y in range(ny):
        w = primitive([now_ref[c, :, y, :] for c in range(fields)])
        first = (lane >= y * seg) & (lane < y * seg + 5)
        mine = (lane >= y * seg) & (lane < (y + 1) * seg)
        for c in range(fields):
            w_ref[y, c] = w[c]
            if y >= ny - ghost:
                up_ref[(y - ny + ghost) * fields + c] = w[c]
            if y < ghost:
                down_ref[y * fields + c] = w[c]
            low = pltpu.roll(w[c], (y * seg + 3) % nx, 1)
            high = pltpu.roll(w[c], (y * seg + 10) % nx, 1)
            edge_ref[c] = jnp.where(mine, jnp.where(first, low, high), edge_ref[c])
        b = primitive([base_ref[c, :, y, :] for c in range(fields)])
        stiff_gamma, stiff_term = mixture(b[6])
        speed = jnp.maximum(jnp.maximum(jnp.abs(b[2]), jnp.abs(b[3])), jnp.abs(b[4]))
        speed = speed + sound(b, b[0] + b[1], stiff_gamma, stiff_term)
        fastest = speed if fastest is None else jnp.maximum(fastest, speed)
    up_ref[ghost * fields] = fastest
    down_ref[ghost * fields] = fastest
    edge_ref[fields] = fastest
    inner = primitive([inflow_ref[c] for c in range(fields)])
    for c in range(fields):
        in_ref[c] = inner[c]


def span_kernel(w_ref, rate_ref):
    ny = w_ref.shape[0]
    nz = w_ref.shape[2]

    def plane(y, _):
        left, right = [], []
        for k in range(fields):
            h = w_ref[y, k]
            c = pltpu.roll(h, nz - 1, 0) - h
            b = pltpu.roll(c, 1, 0)
            a = pltpu.roll(c, 2, 0)
            d = pltpu.roll(c, nz - 1, 0)
            up, down = cell_faces(k, a, b, c, d, h)
            left.append(pltpu.roll(up, 1, 0))
            right.append(down)
        flux = face_flux(left, right, 2)
        diff = [pltpu.roll(f, nz - 1, 0) - f for f in flux]
        for k in range(fields):
            rate_ref[y, k] = -diff[k] if k < 6 else w_ref[y, 6] * diff[7] - diff[6]
        return 0

    lax.fori_loop(0, ny, plane, 0)


def main_kernel(
    place_ref, w_ref, rate_ref, low_ref, high_ref, edge_ref, left_ref, right_ref, in_ref,
    speed_ref, now_ref, base_ref, out_ref,
    tall, ring, sides, seam, flux_ref, keep, acc,
):
    ny, _, nz, nx = w_ref.shape
    seg = nx // ny
    lane = lane_of((nz, nx))
    part = lane % seg
    is_first = place_ref[0] == 1
    is_last = place_ref[1] == 1

    for y in range(ghost):
        for c in range(fields):
            tall[y, c] = low_ref[y * fields + c]
            tall[ghost + ny + y, c] = high_ref[y * fields + c]

    def copy(y, _):
        tall[y + ghost] = w_ref[y]
        return 0

    lax.fori_loop(0, ny, copy, 0)

    def cross(i, _):
        left = [keep[k] for k in range(fields)]
        right = []
        for k in range(fields):
            f, g, h, kk, l = [tall[i + o, k] for o in range(5)]
            up, down = cell_faces(k, g - f, h - g, kk - h, l - kk, h)
            keep[k] = up
            right.append(down)

        @pl.when(i > 0)
        def _():
            flux = face_flux(left, right, 1)

            @pl.when(i > 1)
            def _():
                y = i - 2
                diff = [flux[k] - keep[fields + k] for k in range(fields + 1)]
                for k in range(6):
                    acc[y, k] = rate_ref[y, k] - diff[k]
                acc[y, 6] = rate_ref[y, 6] - diff[6] + w_ref[y, 6] * diff[7]

            for k in range(fields + 1):
                keep[fields + k] = flux[k]

        return 0

    lax.fori_loop(0, ny + 2, cross, 0)

    for k in range(fields):
        e = edge_ref[k]
        last = jnp.where(
            part == 10, pltpu.roll(e, 1, 1), jnp.where(part == 11, pltpu.roll(e, 2, 1), pltpu.roll(e, 3, 1))
        )
        lower = jnp.where(is_first, in_ref[k], left_ref[k])
        upper = jnp.where(is_last, last, right_ref[k])
        e = jnp.where(part < 3, lower, jnp.where((part >= 10) & (part < 13), upper, e))
        c = pltpu.roll(e, nx - 1, 1) - e
        ring[k] = c
        up, down = cell_faces(
            k, pltpu.roll(c, 2, 1), pltpu.roll(c, 1, 1), c, pltpu.roll(c, nx - 1, 1), e
        )
        sides[k] = up
        sides[fields + k] = down

    def stream(y, _):
        base = y * seg
        left, right = [], []
        at_seam = lane == base + 10
        for k in range(fields):
            h = w_ref[y, k]
            de = ring[k]
            tail = pltpu.roll(de, nx - 11 - base, 1)
            head = pltpu.roll(de, nx - 1 - base, 1)
            c = jnp.where(lane == nx - 1, pltpu.roll(tail, 1, 1), pltpu.roll(h, nx - 1, 1) - h)
            d = jnp.where(lane == nx - 1, tail, pltpu.roll(c, nx - 1, 1))
            a = jnp.where(lane < 2, head, pltpu.roll(c, 2, 1))
            b = jnp.where(lane < 1, pltpu.roll(head, nx - 1, 1), pltpu.roll(c, 1, 1))
            up, down = cell_faces(k, a, b, c, d, h)
            seam[k] = jnp.where(at_seam, pltpu.roll(up, base + 11, 1), seam[k])
            edge_up = pltpu.roll(sides[k], nx - base - 2, 1)
            left.append(jnp.where(lane < 1, edge_up, pltpu.roll(up, 1, 1)))
            right.append(down)
        flux = face_flux(left, right, 0)
        for k in range(fields + 1):
            flux_ref[y, k] = flux[k]
        return 0

    lax.fori_loop(0, ny, stream, 0)
    outer = face_flux(
        [seam[k] for k in range(fields)], [sides[fields + k] for k in range(fields)], 0
    )
    for k in range(fields + 1):
        keep[k] = outer[k]

    fastest = jnp.max(speed_ref[...])
    step = courant / jnp.full((nz, nx), fastest, jnp.float32)

    for y in range(ny):
        diff = []
        for k in range(fields + 1):
            f = flux_ref[y, k]
            end = pltpu.roll(keep[k], (2 * nx - 1 - 10 - y * seg) % nx, 1)
            diff.append(jnp.where(lane == nx - 1, end, pltpu.roll(f, nx - 1, 1)) - f)
        for k in range(fields):
            rate = acc[y, k] - diff[k]
            if k == 6:
                rate = rate + w_ref[y, 6] * diff[7]
            out_ref[k, :, y, :] = base_ref[k, :, y, :] * (1.0 / 3.0) + (2.0 / 3.0) * (
                now_ref[k, :, y, :] + step * rate
            )


def tile(count, nz, nx):
    return jax.ShapeDtypeStruct((count, nz, nx), jnp.float32)


def ring_pairs(size, shift):
    return [(i, (i + shift) % size) for i in range(size)]


def shards(state_now, state_base, inflow):
    _, nz, ny, nx = state_now.shape
    seg = nx // ny
    width = ghost * fields + 1
    packed = jnp.pad(inflow, ((0, 0), (0, 0), (0, 0), (0, seg - ghost))).reshape(fields, nz, nx)
    wide = jax.ShapeDtypeStruct((ny, fields, nz, nx), jnp.float32)
    w, up, down, edge, inner = pl.pallas_call(
        pack_kernel,
        out_shape=(
            wide,
            tile(width, nz, nx),
            tile(width, nz, nx),
            tile(fields + 1, nz, nx),
            tile(fields, nz, nx),
        ),
        name="pack",
    )(state_now, state_base, packed)

    streams, crosses = lax.axis_size("stream"), lax.axis_size("cross")
    low = lax.ppermute(up, "cross", ring_pairs(crosses, 1))
    high = lax.ppermute(down, "cross", ring_pairs(crosses, -1))
    left = lax.ppermute(edge, "stream", ring_pairs(streams, 1))
    right = lax.ppermute(edge, "stream", ring_pairs(streams, -1))

    rate = pl.pallas_call(span_kernel, out_shape=wide, name="span")(w)

    speed = jnp.maximum(jnp.maximum(low[-1], high[-1]), edge[-1])
    reach = 3
    while reach < crosses:
        ahead = lax.ppermute(speed, "cross", ring_pairs(crosses, reach))
        behind = lax.ppermute(speed, "cross", ring_pairs(crosses, -reach))
        speed = jnp.maximum(speed, jnp.maximum(ahead, behind))
        reach *= 3
    if streams & (streams - 1) == 0:
        hop = 1
        while hop < streams:
            pairs = [(i, i ^ hop) for i in range(streams)]
            speed = jnp.maximum(speed, lax.ppermute(speed, "stream", pairs))
            hop *= 2
    else:
        speed = functools.reduce(
            jnp.maximum,
            [lax.ppermute(speed, "stream", ring_pairs(streams, s)) for s in range(1, streams)],
            speed,
        )

    position = lax.axis_index("stream")
    place = jnp.stack([position == 0, position == streams - 1]).astype(jnp.int32)
    vmem = pl.BlockSpec(memory_space=pltpu.VMEM)
    return pl.pallas_call(
        main_kernel,
        out_shape=jax.ShapeDtypeStruct(state_now.shape, jnp.float32),
        in_specs=[pl.BlockSpec(memory_space=pltpu.SMEM)] + [vmem] * 11,
        scratch_shapes=[
            pltpu.VMEM((ny + 2 * ghost, fields, nz, nx), jnp.float32),
            pltpu.VMEM((fields, nz, nx), jnp.float32),
            pltpu.VMEM((2 * fields, nz, nx), jnp.float32),
            pltpu.VMEM((fields, nz, nx), jnp.float32),
            pltpu.VMEM((ny, fields + 1, nz, nx), jnp.float32),
            pltpu.VMEM((2 * fields + 1, nz, nx), jnp.float32),
            pltpu.VMEM((ny, fields, nz, nx), jnp.float32),
        ],
        name="sweep",
    )(place, w, rate, low, high, edge, left, right, inner, speed, state_now, state_base)


def solution(mesh):
    return jax.shard_map(
        shards,
        mesh=mesh,
        in_specs=(
            P(None, None, "cross", "stream"),
            P(None, None, "cross", "stream"),
            P(None, None, "cross", None),
        ),
        out_specs=P(None, None, "cross", "stream"),
        check_vma=False,
    )
```

time: 59.2 us -> 38.3 us (0.65)
  the two profiles are of different devices: /device:TPU:0 before, /device:TPU:5 now
where the time goes in v1:
time: 38.3 us; the launch traced here: 38 us
  Pallas kernels  12.5 us (33%)
  starting transfers between devices  11.5 us (30%)
  waiting for transfers between devices  9.42 us (25%)
  local copies, waits for them, and re-layouts  2.63 us (7%)
  other arithmetic  1.95 us (5%)
    pallas_call x1, Pallas kernels, shards(): pl.pallas_call(main_kernel, out_shape=jax.ShapeDtypeStruct(state_now.shap...  7.42 us
    ppermute x1, starting transfers between devices, shards(): behind = lax.ppermute(speed, 'cross', ring_pairs(crosses, -reach))  5.05 us
    ppermute x1, waiting for transfers between devices, shards(): ahead = lax.ppermute(speed, 'cross', ring_pairs(crosses, reach))  4.4 us
    ppermute x2, starting transfers between devices, shards(): speed = jnp.maximum(speed, lax.ppermute(speed, 'stream', pairs))  3.21 us
    pallas_call x1, Pallas kernels, shards(): rate = pl.pallas_call(span_kernel, out_shape=wide, name='span')(w)  2.64 us
    pallas_call x1, Pallas kernels, shards(): pl.pallas_call(pack_kernel, out_shape=(wide, tile(width, nz, nx), tile(wi...  2.49 us
    ppermute x1, waiting for transfers between devices, shards(): high = lax.ppermute(down, 'cross', ring_pairs(crosses, -1))  2.14 us
    ppermute x1, waiting for transfers between devices, shards(): low = lax.ppermute(up, 'cross', ring_pairs(crosses, 1))  2.12 us
  transfers between devices with their start and end apart: 8, of which 4 were waited for; matrix products, arithmetic and copies ran while one was open for 3% of the time, Pallas kernels for 7%

profile of v1, /device:TPU:5, one launch (start us, length us, event | category | flops | bytes accessed | tf_op | source)
XLA Modules:
  0.0 38.0 jit_solution(4316288646736559760)
XLA Ops:
  0.0 1.3 %copy.5 = f32[7,8,8,3]{3,2,1,0:T(8,128)S(1)} copy(f32[7,8,8,3]{2,1,3,0:T(8,128)} %param.5) | data formatting | bytes 10752
  1.3 0.7 %reshape.5.inflow_ref = f32[7,8,128]{2,1,0:T(8,128)} reshape(f32[7,8,8,16]{3,2,1,0:T(8,128)S(1)} %pad.4.clone) | data formatting | bytes 57344 | tf_op jit(solution)/shard_map/reshape | solution.py:290
  2.0 2.5 %pack.1 = (f32[8,7,8,128]{3,2,1,0:T(8,128)}, f32[22,8,128]{2,1,0:T(8,128)}, f32[22,8,128]{2,1,0:T(8,128)}, f32[8,8,128]{2,1,0:T(8,128)}, f32[7,8,128]{2,1,0:T(8,128)}) custom-call(f32[7,8,8,128]{3,2,1,0:T(8,128)} %now_ref.3, f32[7,8,8,128]{3,2,1,0:T(8,128)} %base_ref.3, f32[7,8,128]{2,1,0:T(8,128)} %reshape.5.inflow_ref), custom_call_target="tpu_custom_call" | custom-call | tf_op jit(solution)/shard_map/pack/pallas_call | solution.py:292
  4.5 1.2 %collective-permute-start = (f32[22,8,128]{2,1,0:T(8,128)}, f32[22,8,128]{2,1,0:T(8,128)S(1)}, u32[]{:S(2)}, u32[]{:S(2)}) collective-permute-start(f32[22,8,128]{2,1,0:T(8,128)} %get-tuple-element.11), channel_id=1, source_target_pairs={{0,1},{1,2},{2,3},{3,4},{4,5},{5,6},{6,7},{7,0},{8,9},{9,10},{10,1... | collective-permute-start | bytes 270344 | tf_op jit(solution)/shard_map/ppermute | solution.py:305
  5.8 0.2 collective-permute-start.1
  6.0 2.1 %collective-permute-done.low_ref = f32[22,8,128]{2,1,0:T(8,128)S(1)} collective-permute-done((f32[22,8,128]{2,1,0:T(8,128)}, f32[22,8,128]{2,1,0:T(8,128)S(1)}, u32[]{:S(2)}, u32[]{:S(2)}) %collective-permute-start) | collective-permute-done | bytes 90144 | tf_op jit(solution)/shard_map/ppermute | solution.py:305
  8.1 2.1 %collective-permute-done.1.high_ref = f32[22,8,128]{2,1,0:T(8,128)S(1)} collective-permute-done((f32[22,8,128]{2,1,0:T(8,128)}, f32[22,8,128]{2,1,0:T(8,128)S(1)}, u32[]{:S(2)}, u32[]{:S(2)}) %collective-permute-start.1) | collective-permute-done | bytes 90144 | tf_op jit(solution)/shard_map/ppermute | solution.py:306
  10.2 0.7 %fusion.1 = f32[8,128]{1,0:T(8,128)S(1)} fusion(f32[22,8,128]{2,1,0:T(8,128)S(1)} %collective-permute-done.1.high_ref, f32[22,8,128]{2,1,0:T(8,128)S(1)} %collective-permute-done.low_ref, f32[8,8,128]{2,1,0:T(8,128)} %get-tuple-element.13.edge_ref), kind=kLoop, calls=%fused_computation.2 | loop fusion | flops 2048 | bytes 16384 | tf_op jit(solution)/shard_map/max | solution.py:312
  10.9 5.0 %collective-permute-start.5 = (f32[8,128]{1,0:T(8,128)S(1)}, f32[8,128]{1,0:T(8,128)S(1)}, u32[]{:S(2)}, u32[]{:S(2)}) collective-permute-start(f32[8,128]{1,0:T(8,128)S(1)} %fusion.1), channel_id=1, source_target_pairs={{0,5},{1,6},{2,7},{3,0},{4,1},{5,2},{6,3},{7,4},{8,13},{9,14},{10,... | collective-permute-start | bytes 12296 | tf_op jit(solution)/shard_map/ppermute | solution.py:316
  16.0 0.0 collective-permute-start.4
  16.0 0.8 %collective-permute-done.5 = f32[8,128]{1,0:T(8,128)S(1)} collective-permute-done((f32[8,128]{1,0:T(8,128)S(1)}, f32[8,128]{1,0:T(8,128)S(1)}, u32[]{:S(2)}, u32[]{:S(2)}) %collective-permute-start.5) | collective-permute-done | bytes 4128 | tf_op jit(solution)/shard_map/ppermute | solution.py:316
  16.7 4.4 %collective-permute-done.4 = f32[8,128]{1,0:T(8,128)S(1)} collective-permute-done((f32[8,128]{1,0:T(8,128)S(1)}, f32[8,128]{1,0:T(8,128)S(1)}, u32[]{:S(2)}, u32[]{:S(2)}) %collective-permute-start.4) | collective-permute-done | bytes 4128 | tf_op jit(solution)/shard_map/ppermute | solution.py:315
  21.1 2.0 %collective-permute-start.6 = (f32[8,128]{1,0:T(8,128)S(1)}, f32[8,128]{1,0:T(8,128)S(1)}, u32[]{:S(2)}, u32[]{:S(2)}) collective-permute-start(f32[8,128]{1,0:T(8,128)S(1)} %maximum_maximum_fusion), channel_id=1, source_target_pairs={{0,8},{8,0},{16,24},{24,16},{1,9},{9,1},{17,25},{25,17},{2,10},{10... | collective-permute-start | bytes 12296 | tf_op jit(solution)/shard_map/ppermute | solution.py:323
  23.1 0.1 collective-permute-start.3
  23.2 1.7 %collective-permute-start.2 = (f32[8,8,128]{2,1,0:T(8,128)S(1)}, f32[8,8,128]{2,1,0:T(8,128)S(1)}, u32[]{:S(2)}, u32[]{:S(2)}) collective-permute-start(f32[8,8,128]{2,1,0:T(8,128)S(1)} %copy-done.2), channel_id=1, source_target_pairs={{0,8},{8,16},{16,24},{24,0},{1,9},{9,17},{17,25},{25,1},{2,10},{10... | collective-permute-start | bytes 98312 | tf_op jit(solution)/shard_map/ppermute | solution.py:307
  24.9 0.0 collective-permute-done.6
  24.9 1.2 %collective-permute-start.7 = (f32[8,128]{1,0:T(8,128)S(1)}, f32[8,128]{1,0:T(8,128)S(1)}, u32[]{:S(2)}, u32[]{:S(2)}) collective-permute-start(f32[8,128]{1,0:T(8,128)S(1)} %max.27), channel_id=1, source_target_pairs={{0,16},{8,24},{16,0},{24,8},{1,17},{9,25},{17,1},{25,9},{2,18},{10... | collective-permute-start | bytes 12296 | tf_op jit(solution)/shard_map/ppermute | solution.py:323
  26.1 0.7 %add_convert_fusion.place_ref = s32[2]{0:T(128)} fusion(pred[1]{0:T(512)(128)(4,1)} %bitcast.1, pred[1]{0:T(512)(128)(4,1)} %bitcast), kind=kLoop, calls=%fused_computation.4 | loop fusion | flops 4 | bytes 10 | tf_op jit(solution)/shard_map/convert_element_type | solution.py:333
  26.8 2.6 %span.1.rate_ref = f32[8,7,8,128]{3,2,1,0:T(8,128)} custom-call(f32[8,7,8,128]{3,2,1,0:T(8,128)} %get-tuple-element.10.w_ref), custom_call_target="tpu_custom_call" | custom-call | tf_op jit(solution)/shard_map/span/pallas_call | solution.py:310
  29.4 0.0 collective-permute-done.7
  29.4 0.6 %max.28.speed_ref = f32[8,128]{1,0:T(8,128)} maximum(f32[8,128]{1,0:T(8,128)S(1)} %max.27, f32[8,128]{1,0:T(8,128)S(1)} %collective-permute-done.7) | non-fusion elementwise | flops 1024 | bytes 12288 | tf_op jit(solution)/shard_map/max | solution.py:323
  30.0 0.6 %copy-done.3 = f32[8,8,128]{2,1,0:T(8,128)} copy-done((f32[8,8,128]{2,1,0:T(8,128)}, f32[8,8,128]{2,1,0:T(8,128)S(1)}, u32[]{:S(2)}) %copy-start.3) | copy-done | bytes 32792
  30.6 0.0 copy-done.4
  30.6 7.4 %sweep.1 = f32[7,8,8,128]{3,2,1,0:T(8,128)} custom-call(s32[2]{0:T(128)} %add_convert_fusion.place_ref, f32[8,7,8,128]{3,2,1,0:T(8,128)} %get-tuple-element.10.w_ref, f32[8,7,8,128]{3,2,1,0:T(8,128)} %span.1.rate_ref, f32[22,8,128]{2,1,0:T(8,128)} %copy-done, f32[22,8,128]{2,1,0:T(8,128)} %copy-done.1, f32[8,8,128]{2,1,0:T(8,128)} %get-tuple-element.13.edge_ref, ...), custom_call_target="tpu_custom_call" | custom-call | tf_op jit(solution)/shard_map/sweep/pallas_call | solution.py:335
  (13 shorter events, 0.0 us)
Async XLA Ops:
  4.5 18.6 %copy-start.2 = (f32[8,8,128]{2,1,0:T(8,128)S(1)}, f32[8,8,128]{2,1,0:T(8,128)}, u32[]{:S(2)}) copy-start(f32[8,8,128]{2,1,0:T(8,128)} %get-tuple-element.13.edge_ref) | copy-start | bytes 98308
  4.5 3.6 %collective-permute-start = (f32[22,8,128]{2,1,0:T(8,128)}, f32[22,8,128]{2,1,0:T(8,128)S(1)}, u32[]{:S(2)}, u32[]{:S(2)}) collective-permute-start(f32[22,8,128]{2,1,0:T(8,128)} %get-tuple-element.11), channel_id=1, source_target_pairs={{0,1},{1,2},{2,3},{3,4},{4,5},{5,6},{6,7},{7,0},{8,9},{9,10},{10,1... | collective-permute-start | bytes 270344 | tf_op jit(solution)/shard_map/ppermute | solution.py:305
  5.8 4.5 %collective-permute-start.1 = (f32[22,8,128]{2,1,0:T(8,128)}, f32[22,8,128]{2,1,0:T(8,128)S(1)}, u32[]{:S(2)}, u32[]{:S(2)}) collective-permute-start(f32[22,8,128]{2,1,0:T(8,128)} %get-tuple-element.12), channel_id=1, source_target_pairs={{0,7},{1,0},{2,1},{3,2},{4,3},{5,4},{6,5},{7,6},{8,15},{9,8},{10,9... | collective-permute-start | bytes 270344 | tf_op jit(solution)/shard_map/ppermute | solution.py:306
  8.1 21.3 %copy-start = (f32[22,8,128]{2,1,0:T(8,128)}, f32[22,8,128]{2,1,0:T(8,128)S(1)}, u32[]{:S(2)}) copy-start(f32[22,8,128]{2,1,0:T(8,128)S(1)} %collective-permute-done.low_ref) | copy-start | bytes 270340
  10.2 19.2 %copy-start.1 = (f32[22,8,128]{2,1,0:T(8,128)}, f32[22,8,128]{2,1,0:T(8,128)S(1)}, u32[]{:S(2)}) copy-start(f32[22,8,128]{2,1,0:T(8,128)S(1)} %collective-permute-done.1.high_ref) | copy-start | bytes 270340
  10.9 5.8 %collective-permute-start.5 = (f32[8,128]{1,0:T(8,128)S(1)}, f32[8,128]{1,0:T(8,128)S(1)}, u32[]{:S(2)}, u32[]{:S(2)}) collective-permute-start(f32[8,128]{1,0:T(8,128)S(1)} %fusion.1), channel_id=1, source_target_pairs={{0,5},{1,6},{2,7},{3,0},{4,1},{5,2},{6,3},{7,4},{8,13},{9,14},{10,... | collective-permute-start | bytes 12296 | tf_op jit(solution)/shard_map/ppermute | solution.py:316
  16.0 5.2 %collective-permute-start.4 = (f32[8,128]{1,0:T(8,128)S(1)}, f32[8,128]{1,0:T(8,128)S(1)}, u32[]{:S(2)}, u32[]{:S(2)}) collective-permute-start(f32[8,128]{1,0:T(8,128)S(1)} %fusion.1), channel_id=1, source_target_pairs={{0,3},{1,4},{2,5},{3,6},{4,7},{5,0},{6,1},{7,2},{8,11},{9,12},{10,... | collective-permute-start | bytes 12296 | tf_op jit(solution)/shard_map/ppermute | solution.py:315
  21.1 3.7 %collective-permute-start.6 = (f32[8,128]{1,0:T(8,128)S(1)}, f32[8,128]{1,0:T(8,128)S(1)}, u32[]{:S(2)}, u32[]{:S(2)}) collective-permute-start(f32[8,128]{1,0:T(8,128)S(1)} %maximum_maximum_fusion), channel_id=1, source_target_pairs={{0,8},{8,0},{16,24},{24,16},{1,9},{9,1},{17,25},{25,17},{2,10},{10... | collective-permute-start | bytes 12296 | tf_op jit(solution)/shard_map/ppermute | solution.py:323
  23.1 6.9 %collective-permute-start.3 = (f32[8,8,128]{2,1,0:T(8,128)S(1)}, f32[8,8,128]{2,1,0:T(8,128)S(1)}, u32[]{:S(2)}, u32[]{:S(2)}) collective-permute-start(f32[8,8,128]{2,1,0:T(8,128)S(1)} %copy-done.2), channel_id=1, source_target_pairs={{0,24},{8,0},{16,8},{24,16},{1,25},{9,1},{17,9},{25,17},{2,26},{10... | collective-permute-start | bytes 98312 | tf_op jit(solution)/shard_map/ppermute | solution.py:308
  23.2 6.8 %collective-permute-start.2 = (f32[8,8,128]{2,1,0:T(8,128)S(1)}, f32[8,8,128]{2,1,0:T(8,128)S(1)}, u32[]{:S(2)}, u32[]{:S(2)}) collective-permute-start(f32[8,8,128]{2,1,0:T(8,128)S(1)} %copy-done.2), channel_id=1, source_target_pairs={{0,8},{8,16},{16,24},{24,0},{1,9},{9,17},{17,25},{25,1},{2,10},{10... | collective-permute-start | bytes 98312 | tf_op jit(solution)/shard_map/ppermute | solution.py:307
  24.9 4.5 %collective-permute-start.7 = (f32[8,128]{1,0:T(8,128)S(1)}, f32[8,128]{1,0:T(8,128)S(1)}, u32[]{:S(2)}, u32[]{:S(2)}) collective-permute-start(f32[8,128]{1,0:T(8,128)S(1)} %max.27), channel_id=1, source_target_pairs={{0,16},{8,24},{16,0},{24,8},{1,17},{9,25},{17,1},{25,9},{2,18},{10... | collective-permute-start | bytes 12296 | tf_op jit(solution)/shard_map/ppermute | solution.py:323
  30.0 0.6 %copy-start.3 = (f32[8,8,128]{2,1,0:T(8,128)}, f32[8,8,128]{2,1,0:T(8,128)S(1)}, u32[]{:S(2)}) copy-start(f32[8,8,128]{2,1,0:T(8,128)S(1)} %collective-permute-done.3.right_ref) | copy-start | bytes 98308
  30.0 0.6 %copy-start.4 = (f32[8,8,128]{2,1,0:T(8,128)}, f32[8,8,128]{2,1,0:T(8,128)S(1)}, u32[]{:S(2)}) copy-start(f32[8,8,128]{2,1,0:T(8,128)S(1)} %collective-permute-done.2.left_ref) | copy-start | bytes 98308

commit v2 on v1

--- a/solution.py
+++ b/solution.py
@@ -1,5 +1,3 @@
-import functools
-
 import jax
 import jax.numpy as jnp
 from jax import lax
@@ -103,7 +101,7 @@
     return lax.broadcasted_iota(jnp.int32, shape, 1)
 
 
-def pack_kernel(now_ref, base_ref, inflow_ref, w_ref, up_ref, down_ref, edge_ref, in_ref):
+def pack_kernel(now_ref, base_ref, w_ref, up_ref, down_ref, edge_ref):
     nz, ny, nx = now_ref.shape[1:]
     seg = nx // ny
     lane = lane_of((nz, nx))
@@ -131,14 +129,11 @@
     up_ref[ghost * fields] = fastest
     down_ref[ghost * fields] = fastest
     edge_ref[fields] = fastest
-    inner = primitive([inflow_ref[c] for c in range(fields)])
-    for c in range(fields):
-        in_ref[c] = inner[c]
-
-
-def span_kernel(w_ref, rate_ref):
-    ny = w_ref.shape[0]
-    nz = w_ref.shape[2]
+
+
+def span_kernel(w_ref, inflow_ref, rate_ref, in_ref):
+    ny, _, nz, nx = w_ref.shape
+    seg = nx // ny
 
     def plane(y, _):
         left, right = [], []
@@ -159,11 +154,70 @@
 
     lax.fori_loop(0, ny, plane, 0)
 
-
-def main_kernel(
-    place_ref, w_ref, rate_ref, low_ref, high_ref, edge_ref, left_ref, right_ref, in_ref,
-    speed_ref, now_ref, base_ref, out_ref,
-    tall, ring, sides, seam, flux_ref, keep, acc,
+    lane = lane_of((nz, nx))
+    layers = []
+    for c in range(fields):
+        packed = jnp.ones((nz, nx), jnp.float32)
+        for g in range(ghost):
+            layer = jnp.concatenate(
+                [inflow_ref[c, g], jnp.zeros((nz, nx - ny), jnp.float32)], axis=1
+            )
+            for y in range(ny):
+                shift = (y * seg + g - y) % nx
+                moved = layer if shift == 0 else pltpu.roll(layer, shift, 1)
+                packed = jnp.where(lane == y * seg + g, moved, packed)
+        layers.append(packed)
+    layers = primitive(layers)
+    for c in range(fields):
+        in_ref[c] = layers[c]
+
+
+def cross_kernel(w_ref, rate_ref, low_ref, high_ref, acc, tall, keep):
+    ny = w_ref.shape[0]
+
+    for y in range(ghost):
+        for c in range(fields):
+            tall[y, c] = low_ref[y * fields + c]
+            tall[ghost + ny + y, c] = high_ref[y * fields + c]
+
+    def copy(y, _):
+        tall[y + ghost] = w_ref[y]
+        return 0
+
+    lax.fori_loop(0, ny, copy, 0)
+
+    def cross(i, _):
+        left = [keep[k] for k in range(fields)]
+        right = []
+        for k in range(fields):
+            f, g, h, kk, l = [tall[i + o, k] for o in range(5)]
+            up, down = cell_faces(k, g - f, h - g, kk - h, l - kk, h)
+            keep[k] = up
+            right.append(down)
+
+        @pl.when(i > 0)
+        def _():
+            flux = face_flux(left, right, 1)
+
+            @pl.when(i > 1)
+            def _():
+                y = i - 2
+                diff = [flux[k] - keep[fields + k] for k in range(fields + 1)]
+                for k in range(6):
+                    acc[y, k] = rate_ref[y, k] - diff[k]
+                acc[y, 6] = rate_ref[y, 6] - diff[6] + w_ref[y, 6] * diff[7]
+
+            for k in range(fields + 1):
+                keep[fields + k] = flux[k]
+
+        return 0
+
+    lax.fori_loop(0, ny + 2, cross, 0)
+
+
+def stream_kernel(
+    place_ref, w_ref, edge_ref, left_ref, right_ref, in_ref, acc_ref, rate_ref,
+    ring, sides, seam, flux_ref, keep,
 ):
     ny, _, nz, nx = w_ref.shape
     seg = nx // ny
@@ -171,45 +225,6 @@
     part = lane % seg
     is_first = place_ref[0] == 1
     is_last = place_ref[1] == 1
-
-    for y in range(ghost):
-        for c in range(fields):
-            tall[y, c] = low_ref[y * fields + c]
-            tall[ghost + ny + y, c] = high_ref[y * fields + c]
-
-    def copy(y, _):
-        tall[y + ghost] = w_ref[y]
-        return 0
-
-    lax.fori_loop(0, ny, copy, 0)
-
-    def cross(i, _):
-        left = [keep[k] for k in range(fields)]
-        right = []
-        for k in range(fields):
-            f, g, h, kk, l = [tall[i + o, k] for o in range(5)]
-            up, down = cell_faces(k, g - f, h - g, kk - h, l - kk, h)
-            keep[k] = up
-            right.append(down)
-
-        @pl.when(i > 0)
-        def _():
-            flux = face_flux(left, right, 1)
-
-            @pl.when(i > 1)
-            def _():
-                y = i - 2
-                diff = [flux[k] - keep[fields + k] for k in range(fields + 1)]
-                for k in range(6):
-                    acc[y, k] = rate_ref[y, k] - diff[k]
-                acc[y, 6] = rate_ref[y, 6] - diff[6] + w_ref[y, 6] * diff[7]
-
-            for k in range(fields + 1):
-                keep[fields + k] = flux[k]
-
-        return 0
-
-    lax.fori_loop(0, ny + 2, cross, 0)
 
     for k in range(fields):
         e = edge_ref[k]
@@ -257,9 +272,6 @@
     for k in range(fields + 1):
         keep[k] = outer[k]
 
-    fastest = jnp.max(speed_ref[...])
-    step = courant / jnp.full((nz, nx), fastest, jnp.float32)
-
     for y in range(ny):
         diff = []
         for k in range(fields + 1):
@@ -267,39 +279,53 @@
             end = pltpu.roll(keep[k], (2 * nx - 1 - 10 - y * seg) % nx, 1)
             diff.append(jnp.where(lane == nx - 1, end, pltpu.roll(f, nx - 1, 1)) - f)
         for k in range(fields):
-            rate = acc[y, k] - diff[k]
+            rate = acc_ref[y, k] - diff[k]
             if k == 6:
                 rate = rate + w_ref[y, 6] * diff[7]
-            out_ref[k, :, y, :] = base_ref[k, :, y, :] * (1.0 / 3.0) + (2.0 / 3.0) * (
-                now_ref[k, :, y, :] + step * rate
-            )
-
-
-def tile(count, nz, nx):
-    return jax.ShapeDtypeStruct((count, nz, nx), jnp.float32)
+            rate_ref[y, k] = rate
+
+
+def update_kernel(rate_ref, mine_ref, peer_ref, now_ref, base_ref, out_ref):
+    ny, _, nz, nx = rate_ref.shape
+    fastest = jnp.max(jnp.maximum(mine_ref[...], peer_ref[...]))
+    step = (2.0 / 3.0) * (courant / jnp.full((nz, nx), fastest, jnp.float32))
+    for y in range(ny):
+        for k in range(fields):
+            old = base_ref[k, :, y, :] * (1.0 / 3.0) + (2.0 / 3.0) * now_ref[k, :, y, :]
+            out_ref[k, :, y, :] = old + step * rate_ref[y, k]
+
+
+def buffer(*shape):
+    return pltpu.VMEM(shape, jnp.float32)
+
+
+def near(*arrays):
+    return [pltpu.with_memory_space_constraint(x, pltpu.VMEM) for x in arrays]
 
 
 def ring_pairs(size, shift):
     return [(i, (i + shift) % size) for i in range(size)]
 
 
+def hop_pairs(size, hop, shift):
+    if size & (size - 1) == 0 and size > 1:
+        return [(i, i ^ hop) for i in range(size)]
+    return ring_pairs(size, shift)
+
+
 def shards(state_now, state_base, inflow):
     _, nz, ny, nx = state_now.shape
-    seg = nx // ny
     width = ghost * fields + 1
-    packed = jnp.pad(inflow, ((0, 0), (0, 0), (0, 0), (0, seg - ghost))).reshape(fields, nz, nx)
-    wide = jax.ShapeDtypeStruct((ny, fields, nz, nx), jnp.float32)
-    w, up, down, edge, inner = pl.pallas_call(
+    wide = buffer(ny, fields, nz, nx)
+    vmem = pl.BlockSpec(memory_space=pltpu.VMEM)
+    state_now, state_base = near(state_now, state_base)
+    w, up, down, edge = pl.pallas_call(
         pack_kernel,
-        out_shape=(
-            wide,
-            tile(width, nz, nx),
-            tile(width, nz, nx),
-            tile(fields + 1, nz, nx),
-            tile(fields, nz, nx),
-        ),
+        out_shape=(wide, buffer(width, nz, nx), buffer(width, nz, nx), buffer(fields + 1, nz, nx)),
+        in_specs=[vmem] * 2,
+        out_specs=(vmem,) * 4,
         name="pack",
-    )(state_now, state_base, packed)
+    )(state_now, state_base)
 
     streams, crosses = lax.axis_size("stream"), lax.axis_size("cross")
     low = lax.ppermute(up, "cross", ring_pairs(crosses, 1))
@@ -307,46 +333,70 @@
     left = lax.ppermute(edge, "stream", ring_pairs(streams, 1))
     right = lax.ppermute(edge, "stream", ring_pairs(streams, -1))
 
-    rate = pl.pallas_call(span_kernel, out_shape=wide, name="span")(w)
+    rate, inner = pl.pallas_call(
+        span_kernel,
+        out_shape=(wide, buffer(fields, nz, nx)),
+        in_specs=[vmem] * 2,
+        out_specs=(vmem,) * 2,
+        name="span",
+    )(*near(w, jnp.transpose(inflow, (0, 3, 1, 2))))
+
+    position = lax.axis_index("stream")
+    place = jnp.stack([position == 0, position == streams - 1]).astype(jnp.int32)
+
+    def cross_sweep():
+        return pl.pallas_call(
+            cross_kernel,
+            out_shape=wide,
+            in_specs=[vmem] * 4,
+            out_specs=vmem,
+            scratch_shapes=[
+                buffer(ny + 2 * ghost, fields, nz, nx),
+                buffer(2 * fields + 1, nz, nx),
+            ],
+            name="cross",
+        )(*near(w, rate, low, high))
+
+    def stream_sweep(acc):
+        return pl.pallas_call(
+            stream_kernel,
+            out_shape=wide,
+            in_specs=[pl.BlockSpec(memory_space=pltpu.SMEM)] + [vmem] * 6,
+            out_specs=vmem,
+            scratch_shapes=[
+                buffer(fields, nz, nx),
+                buffer(2 * fields, nz, nx),
+                buffer(fields, nz, nx),
+                buffer(ny, fields + 1, nz, nx),
+                buffer(fields + 1, nz, nx),
+            ],
+            name="stream",
+        )(place, *near(w, edge, left, right, inner, acc))
 
     speed = jnp.maximum(jnp.maximum(low[-1], high[-1]), edge[-1])
+    speed, rate = lax.optimization_barrier((speed, rate))
     reach = 3
     while reach < crosses:
         ahead = lax.ppermute(speed, "cross", ring_pairs(crosses, reach))
         behind = lax.ppermute(speed, "cross", ring_pairs(crosses, -reach))
         speed = jnp.maximum(speed, jnp.maximum(ahead, behind))
         reach *= 3
-    if streams & (streams - 1) == 0:
-        hop = 1
-        while hop < streams:
-            pairs = [(i, i ^ hop) for i in range(streams)]
-            speed = jnp.maximum(speed, lax.ppermute(speed, "stream", pairs))
-            hop *= 2
-    else:
-        speed = functools.reduce(
-            jnp.maximum,
-            [lax.ppermute(speed, "stream", ring_pairs(streams, s)) for s in range(1, streams)],
-            speed,
-        )
-
-    position = lax.axis_index("stream")
-    place = jnp.stack([position == 0, position == streams - 1]).astype(jnp.int32)
-    vmem = pl.BlockSpec(memory_space=pltpu.VMEM)
+    acc = cross_sweep()
+    hop = 1
+    while 2 * hop < streams:
+        pairs = hop_pairs(streams, hop, hop)
+        speed = jnp.maximum(speed, lax.ppermute(speed, "stream", pairs))
+        hop *= 2
+    speed, acc = lax.optimization_barrier((speed, acc))
+    peer = lax.ppermute(speed, "stream", hop_pairs(streams, hop, streams - hop))
+    rate = stream_sweep(acc)
     return pl.pallas_call(
-        main_kernel,
+        update_kernel,
         out_shape=jax.ShapeDtypeStruct(state_now.shape, jnp.float32),
-        in_specs=[pl.BlockSpec(memory_space=pltpu.SMEM)] + [vmem] * 11,
-        scratch_shapes=[
-            pltpu.VMEM((ny + 2 * ghost, fields, nz, nx), jnp.float32),
-            pltpu.VMEM((fields, nz, nx), jnp.float32),
-            pltpu.VMEM((2 * fields, nz, nx), jnp.float32),
-            pltpu.VMEM((fields, nz, nx), jnp.float32),
-            pltpu.VMEM((ny, fields + 1, nz, nx), jnp.float32),
-            pltpu.VMEM((2 * fields + 1, nz, nx), jnp.float32),
-            pltpu.VMEM((ny, fields, nz, nx), jnp.float32),
-        ],
-        name="sweep",
-    )(place, w, rate, low, high, edge, left, right, inner, speed, state_now, state_base)
+        in_specs=[vmem] * 5,
+        out_specs=vmem,
+        name="update",
+    )(*near(rate, speed, peer, state_now, state_base))
 
 
 def solution(mesh):

time: 38.3 us -> 29.4 us (0.77)
  the two profiles are of different devices: /device:TPU:5 before, /device:TPU:0 now
where the time goes in v2:
time: 29.4 us; the launch traced here: 29.3 us
  starting transfers between devices  13.3 us (45%)
  Pallas kernels  9.1 us (31%)
  waiting for transfers between devices  4.3 us (15%)
  local copies, waits for them, and re-layouts  1.88 us (6%)
  other arithmetic  0.63 us (2%)
    pallas_call x1, Pallas kernels, stream_sweep(): pl.pallas_call(stream_kernel, out_shape=wide, in_specs=[pl.BlockSpec(memo...  4.39 us
    ppermute x1, starting transfers between devices, shards(): high = lax.ppermute(down, 'cross', ring_pairs(crosses, -1))  3.1 us
    ppermute x1, starting transfers between devices, shards(): low = lax.ppermute(up, 'cross', ring_pairs(crosses, 1))  3.05 us
    ppermute x1, starting transfers between devices, shards(): behind = lax.ppermute(speed, 'cross', ring_pairs(crosses, -reach))  2.32 us
    unnamed x8, local copies, waits for them, and re-layouts  1.88 us
    ppermute x1, waiting for transfers between devices, shards(): ahead = lax.ppermute(speed, 'cross', ring_pairs(crosses, reach))  1.58 us
    ppermute x1, starting transfers between devices, shards(): peer = lax.ppermute(speed, 'stream', hop_pairs(streams, hop, streams - hop))  1.56 us
    ppermute x1, starting transfers between devices, shards(): ahead = lax.ppermute(speed, 'cross', ring_pairs(crosses, reach))  1.5 us
  transfers between devices with their start and end apart: 8, of which 4 were waited for; matrix products, arithmetic and copies ran while one was open for 2% of the time, Pallas kernels for 24%

profile of v2, /device:TPU:0, one launch (start us, length us, event | category | flops | bytes accessed | tf_op | source)
XLA Modules:
  0.0 29.3 jit_solution(8153042687452293852)
XLA Ops:
  0.0 0.9 %copy-done = f32[7,8,8,128]{3,2,1,0:T(8,128)S(1)} copy-done((f32[7,8,8,128]{3,2,1,0:T(8,128)S(1)}, f32[7,8,8,128]{3,2,1,0:T(8,128)}, u32[]{:S(2)}) %copy-start) | copy-done | bytes 229400
  0.9 0.9 %copy-done.1 = f32[7,8,8,128]{3,2,1,0:T(8,128)S(1)} copy-done((f32[7,8,8,128]{3,2,1,0:T(8,128)S(1)}, f32[7,8,8,128]{3,2,1,0:T(8,128)}, u32[]{:S(2)}) %copy-start.1) | copy-done | bytes 229400
  1.9 0.8 %pack.1 = (f32[8,7,8,128]{3,2,1,0:T(8,128)S(1)}, f32[22,8,128]{2,1,0:T(8,128)S(1)}, f32[22,8,128]{2,1,0:T(8,128)S(1)}, f32[8,8,128]{2,1,0:T(8,128)S(1)}) custom-call(f32[7,8,8,128]{3,2,1,0:T(8,128)S(1)} %copy-done, f32[7,8,8,128]{3,2,1,0:T(8,128)S(1)} %copy-done.1), custom_call_target="tpu_custom_call" | custom-call | tf_op jit(solution)/shard_map/pack/pallas_call | solution.py:322
  2.7 3.0 %collective-permute-start.2 = (f32[22,8,128]{2,1,0:T(8,128)S(1)}, f32[22,8,128]{2,1,0:T(8,128)S(1)}, u32[]{:S(2)}, u32[]{:S(2)}) collective-permute-start(f32[22,8,128]{2,1,0:T(8,128)S(1)} %get-tuple-element.18), channel_id=1, source_target_pairs={{0,1},{1,2},{2,3},{3,4},{4,5},{5,6},{6,7},{7,0},{8,9},{9,10},{10,1... | collective-permute-start | bytes 270344 | tf_op jit(solution)/shard_map/ppermute | solution.py:331
  5.7 3.1 %collective-permute-start.3 = (f32[22,8,128]{2,1,0:T(8,128)S(1)}, f32[22,8,128]{2,1,0:T(8,128)S(1)}, u32[]{:S(2)}, u32[]{:S(2)}) collective-permute-start(f32[22,8,128]{2,1,0:T(8,128)S(1)} %get-tuple-element.19), channel_id=1, source_target_pairs={{0,7},{1,0},{2,1},{3,2},{4,3},{5,4},{6,5},{7,6},{8,15},{9,8},{10,9... | collective-permute-start | bytes 270344 | tf_op jit(solution)/shard_map/ppermute | solution.py:332
  8.8 1.2 %span.1 = (f32[8,7,8,128]{3,2,1,0:T(8,128)S(1)}, f32[7,8,128]{2,1,0:T(8,128)S(1)}) custom-call(f32[8,7,8,128]{3,2,1,0:T(8,128)S(1)} %get-tuple-element.15.w_ref, f32[7,3,8,8]{3,2,1,0:T(8,128)S(1)} %bitcast.5), custom_call_target="tpu_custom_call" | custom-call | tf_op jit(solution)/shard_map/span/pallas_call | solution.py:336
  10.1 1.4 %collective-permute-done.2.low_ref = f32[22,8,128]{2,1,0:T(8,128)S(1)} collective-permute-done((f32[22,8,128]{2,1,0:T(8,128)S(1)}, f32[22,8,128]{2,1,0:T(8,128)S(1)}, u32[]{:S(2)}, u32[]{:S(2)}) %collective-permute-start.2) | collective-permute-done | bytes 90144 | tf_op jit(solution)/shard_map/ppermute | solution.py:331
  11.5 0.7 %collective-permute-done.3.high_ref = f32[22,8,128]{2,1,0:T(8,128)S(1)} collective-permute-done((f32[22,8,128]{2,1,0:T(8,128)S(1)}, f32[22,8,128]{2,1,0:T(8,128)S(1)}, u32[]{:S(2)}, u32[]{:S(2)}) %collective-permute-start.3) | collective-permute-done | bytes 90144 | tf_op jit(solution)/shard_map/ppermute | solution.py:332
  12.2 1.5 %collective-permute-start.4 = (f32[8,128]{1,0:T(8,128)S(1)}, f32[8,128]{1,0:T(8,128)S(1)}, u32[]{:S(2)}, u32[]{:S(2)}) collective-permute-start(f32[8,128]{1,0:T(8,128)S(1)} %fusion.1), channel_id=1, source_target_pairs={{0,3},{1,4},{2,5},{3,6},{4,7},{5,0},{6,1},{7,2},{8,11},{9,12},{10,... | collective-permute-start | bytes 12296 | tf_op jit(solution)/shard_map/ppermute | solution.py:380
  13.7 2.3 %collective-permute-start.5 = (f32[8,128]{1,0:T(8,128)S(1)}, f32[8,128]{1,0:T(8,128)S(1)}, u32[]{:S(2)}, u32[]{:S(2)}) collective-permute-start(f32[8,128]{1,0:T(8,128)S(1)} %fusion.1), channel_id=1, source_target_pairs={{0,5},{1,6},{2,7},{3,0},{4,1},{5,2},{6,3},{7,4},{8,13},{9,14},{10,... | collective-permute-start | bytes 12296 | tf_op jit(solution)/shard_map/ppermute | solution.py:381
  16.0 1.6 %collective-permute-done.4 = f32[8,128]{1,0:T(8,128)S(1)} collective-permute-done((f32[8,128]{1,0:T(8,128)S(1)}, f32[8,128]{1,0:T(8,128)S(1)}, u32[]{:S(2)}, u32[]{:S(2)}) %collective-permute-start.4) | collective-permute-done | bytes 4128 | tf_op jit(solution)/shard_map/ppermute | solution.py:380
  17.6 0.6 %collective-permute-done.5 = f32[8,128]{1,0:T(8,128)S(1)} collective-permute-done((f32[8,128]{1,0:T(8,128)S(1)}, f32[8,128]{1,0:T(8,128)S(1)}, u32[]{:S(2)}, u32[]{:S(2)}) %collective-permute-start.5) | collective-permute-done | bytes 4128 | tf_op jit(solution)/shard_map/ppermute | solution.py:381
  18.2 0.0 collective-permute-start.6
  18.2 0.5 %collective-permute-start = (f32[8,8,128]{2,1,0:T(8,128)S(1)}, f32[8,8,128]{2,1,0:T(8,128)S(1)}, u32[]{:S(2)}, u32[]{:S(2)}) collective-permute-start(f32[8,8,128]{2,1,0:T(8,128)S(1)} %get-tuple-element.16.edge_ref), channel_id=1, source_target_pairs={{0,8},{8,16},{16,24},{24,0},{1,9},{9,17},{17,25},{25,1},{2,10},{10... | collective-permute-start | bytes 98312 | tf_op jit(solution)/shard_map/ppermute | solution.py:333
  18.7 1.2 %collective-permute-start.1 = (f32[8,8,128]{2,1,0:T(8,128)S(1)}, f32[8,8,128]{2,1,0:T(8,128)S(1)}, u32[]{:S(2)}, u32[]{:S(2)}) collective-permute-start(f32[8,8,128]{2,1,0:T(8,128)S(1)} %get-tuple-element.16.edge_ref), channel_id=1, source_target_pairs={{0,24},{8,0},{16,8},{24,16},{1,25},{9,1},{17,9},{25,17},{2,26},{10... | collective-permute-start | bytes 98312 | tf_op jit(solution)/shard_map/ppermute | solution.py:334
  19.9 1.4 %cross.1.acc_ref = f32[8,7,8,128]{3,2,1,0:T(8,128)S(1)} custom-call(f32[8,7,8,128]{3,2,1,0:T(8,128)S(1)} %get-tuple-element.15.w_ref, f32[8,7,8,128]{3,2,1,0:T(8,128)S(1)} %get-tuple-element.22.rate_ref, f32[22,8,128]{2,1,0:T(8,128)S(1)} %collective-permute-done.2.low_ref, f32[22,8,128]{2,1,0:T(8,128)S(1)} %collective-permute-done.3.high_ref), custom_call_target="tpu_custom_call" | custom-call | tf_op jit(solution)/shard_map/cross/pallas_call | solution.py:348
  21.4 0.0 collective-permute-done.6
  21.4 1.6 %collective-permute-start.7 = (f32[8,128]{1,0:T(8,128)S(1)}, f32[8,128]{1,0:T(8,128)S(1)}, u32[]{:S(2)}, u32[]{:S(2)}) collective-permute-start(f32[8,128]{1,0:T(8,128)S(1)} %max.24.mine_ref), channel_id=1, source_target_pairs={{0,16},{8,24},{16,0},{24,8},{1,17},{9,25},{17,1},{25,9},{2,18},{10... | collective-permute-start | bytes 12296 | tf_op jit(solution)/shard_map/ppermute | solution.py:391
  23.0 0.6 %add_convert_fusion.place_ref = s32[2]{0:T(128)} fusion(pred[1]{0:T(512)(128)(4,1)} %bitcast.1, pred[1]{0:T(512)(128)(4,1)} %bitcast), kind=kLoop, calls=%fused_computation.4 | loop fusion | flops 4 | bytes 10 | tf_op jit(solution)/shard_map/convert_element_type | solution.py:345
  23.6 0.0 collective-permute-done.left_ref
  23.6 0.0 collective-permute-done.1.right_ref
  23.6 4.4 %stream.1.rate_ref = f32[8,7,8,128]{3,2,1,0:T(8,128)S(1)} custom-call(s32[2]{0:T(128)} %add_convert_fusion.place_ref, f32[8,7,8,128]{3,2,1,0:T(8,128)S(1)} %get-tuple-element.15.w_ref, f32[8,8,128]{2,1,0:T(8,128)S(1)} %get-tuple-element.16.edge_ref, f32[8,8,128]{2,1,0:T(8,128)S(1)} %collective-permute-done.left_ref, ...), custom_call_target="tpu_custom_call" | custom-call | tf_op jit(solution)/shard_map/stream/pallas_call | solution.py:361
  28.0 0.0 collective-permute-done.7.peer_ref
  28.0 1.2 %update.1 = f32[7,8,8,128]{3,2,1,0:T(8,128)} custom-call(f32[8,7,8,128]{3,2,1,0:T(8,128)S(1)} %stream.1.rate_ref, f32[8,128]{1,0:T(8,128)S(1)} %max.24.mine_ref, f32[8,128]{1,0:T(8,128)S(1)} %collective-permute-done.7.peer_ref, f32[7,8,8,128]{3,2,1,0:T(8,128)S(1)} %copy-done, f32[7,8,8,128]{3,2,1,0:T(8,128)S(1)} %copy-done.2), custom_call_target="tpu_custom_call" | custom-call | tf_op jit(solution)/shard_map/update/pallas_call | solution.py:393
  (9 shorter events, 0.0 us)
Async XLA Ops:
  0.0 0.9 %copy-start = (f32[7,8,8,128]{3,2,1,0:T(8,128)S(1)}, f32[7,8,8,128]{3,2,1,0:T(8,128)}, u32[]{:S(2)}) copy-start(f32[7,8,8,128]{3,2,1,0:T(8,128)} %now_ref.3) | copy-start | bytes 688132
  0.9 0.9 %copy-start.1 = (f32[7,8,8,128]{3,2,1,0:T(8,128)S(1)}, f32[7,8,8,128]{3,2,1,0:T(8,128)}, u32[]{:S(2)}) copy-start(f32[7,8,8,128]{3,2,1,0:T(8,128)} %base_ref.3) | copy-start | bytes 688132
  1.9 6.9 %copy-start.3 = (f32[7,8,8,3]{2,1,3,0:T(8,128)S(1)}, f32[7,8,8,3]{2,1,3,0:T(8,128)}, u32[]{:S(2)}) copy-start(f32[7,8,8,3]{2,1,3,0:T(8,128)} %param.5) | copy-start | bytes 16132
  2.7 8.8 %collective-permute-start.2 = (f32[22,8,128]{2,1,0:T(8,128)S(1)}, f32[22,8,128]{2,1,0:T(8,128)S(1)}, u32[]{:S(2)}, u32[]{:S(2)}) collective-permute-start(f32[22,8,128]{2,1,0:T(8,128)S(1)} %get-tuple-element.18), channel_id=1, source_target_pairs={{0,1},{1,2},{2,3},{3,4},{4,5},{5,6},{6,7},{7,0},{8,9},{9,10},{10,1... | collective-permute-start | bytes 270344 | tf_op jit(solution)/shard_map/ppermute | solution.py:331
  5.7 6.5 %collective-permute-start.3 = (f32[22,8,128]{2,1,0:T(8,128)S(1)}, f32[22,8,128]{2,1,0:T(8,128)S(1)}, u32[]{:S(2)}, u32[]{:S(2)}) collective-permute-start(f32[22,8,128]{2,1,0:T(8,128)S(1)} %get-tuple-element.19), channel_id=1, source_target_pairs={{0,7},{1,0},{2,1},{3,2},{4,3},{5,4},{6,5},{7,6},{8,15},{9,8},{10,9... | collective-permute-start | bytes 270344 | tf_op jit(solution)/shard_map/ppermute | solution.py:332
  12.2 5.4 %collective-permute-start.4 = (f32[8,128]{1,0:T(8,128)S(1)}, f32[8,128]{1,0:T(8,128)S(1)}, u32[]{:S(2)}, u32[]{:S(2)}) collective-permute-start(f32[8,128]{1,0:T(8,128)S(1)} %fusion.1), channel_id=1, source_target_pairs={{0,3},{1,4},{2,5},{3,6},{4,7},{5,0},{6,1},{7,2},{8,11},{9,12},{10,... | collective-permute-start | bytes 12296 | tf_op jit(solution)/shard_map/ppermute | solution.py:380
  13.7 4.5 %collective-permute-start.5 = (f32[8,128]{1,0:T(8,128)S(1)}, f32[8,128]{1,0:T(8,128)S(1)}, u32[]{:S(2)}, u32[]{:S(2)}) collective-permute-start(f32[8,128]{1,0:T(8,128)S(1)} %fusion.1), channel_id=1, source_target_pairs={{0,5},{1,6},{2,7},{3,0},{4,1},{5,2},{6,3},{7,4},{8,13},{9,14},{10,... | collective-permute-start | bytes 12296 | tf_op jit(solution)/shard_map/ppermute | solution.py:381
  18.2 3.2 %collective-permute-start.6 = (f32[8,128]{1,0:T(8,128)S(1)}, f32[8,128]{1,0:T(8,128)S(1)}, u32[]{:S(2)}, u32[]{:S(2)}) collective-permute-start(f32[8,128]{1,0:T(8,128)S(1)} %maximum_maximum_fusion), channel_id=1, source_target_pairs={{0,8},{8,0},{16,24},{24,16},{1,9},{9,1},{17,25},{25,17},{2,10},{10... | collective-permute-start | bytes 12296 | tf_op jit(solution)/shard_map/ppermute | solution.py:388
  18.2 5.4 %collective-permute-start = (f32[8,8,128]{2,1,0:T(8,128)S(1)}, f32[8,8,128]{2,1,0:T(8,128)S(1)}, u32[]{:S(2)}, u32[]{:S(2)}) collective-permute-start(f32[8,8,128]{2,1,0:T(8,128)S(1)} %get-tuple-element.16.edge_ref), channel_id=1, source_target_pairs={{0,8},{8,16},{16,24},{24,0},{1,9},{9,17},{17,25},{25,1},{2,10},{10... | collective-permute-start | bytes 98312 | tf_op jit(solution)/shard_map/ppermute | solution.py:333
  18.7 4.9 %collective-permute-start.1 = (f32[8,8,128]{2,1,0:T(8,128)S(1)}, f32[8,8,128]{2,1,0:T(8,128)S(1)}, u32[]{:S(2)}, u32[]{:S(2)}) collective-permute-start(f32[8,8,128]{2,1,0:T(8,128)S(1)} %get-tuple-element.16.edge_ref), channel_id=1, source_target_pairs={{0,24},{8,0},{16,8},{24,16},{1,25},{9,1},{17,9},{25,17},{2,26},{10... | collective-permute-start | bytes 98312 | tf_op jit(solution)/shard_map/ppermute | solution.py:334
  21.4 6.6 %collective-permute-start.7 = (f32[8,128]{1,0:T(8,128)S(1)}, f32[8,128]{1,0:T(8,128)S(1)}, u32[]{:S(2)}, u32[]{:S(2)}) collective-permute-start(f32[8,128]{1,0:T(8,128)S(1)} %max.24.mine_ref), channel_id=1, source_target_pairs={{0,16},{8,24},{16,0},{24,8},{1,17},{9,25},{17,1},{25,9},{2,18},{10... | collective-permute-start | bytes 12296 | tf_op jit(solution)/shard_map/ppermute | solution.py:391
  23.6 4.4 %copy-start.2 = (f32[7,8,8,128]{3,2,1,0:T(8,128)S(1)}, f32[7,8,8,128]{3,2,1,0:T(8,128)}, u32[]{:S(2)}) copy-start(f32[7,8,8,128]{3,2,1,0:T(8,128)} %base_ref.3) | copy-start | bytes 688132

commit v3 on v2

--- a/solution.py
+++ b/solution.py
@@ -101,16 +101,24 @@
     return lax.broadcasted_iota(jnp.int32, shape, 1)
 
 
-def pack_kernel(now_ref, base_ref, w_ref, up_ref, down_ref, edge_ref):
+def pack_kernel(
+    now_hbm, base_hbm, w_ref, up_ref, down_ref, edge_ref, old_ref, now_ref, base_ref, sems
+):
     nz, ny, nx = now_ref.shape[1:]
     seg = nx // ny
     lane = lane_of((nz, nx))
 
-    edge_ref[...] = jnp.zeros(edge_ref.shape, jnp.float32)
-    fastest = None
+    loads = []
+    for i, (src, dst) in enumerate(((now_hbm, now_ref), (base_hbm, base_ref))):
+        for c in range(fields):
+            loads.append(pltpu.make_async_copy(src.at[c], dst.at[c], sems.at[i * fields + c]))
+    for load in loads:
+        load.start()
+    for load in loads[:fields]:
+        load.wait()
     for y in range(ny):
         w = primitive([now_ref[c, :, y, :] for c in range(fields)])
-        first = (lane >= y * seg) & (lane < y * seg + 5)
+        first = (lane >= y * seg) & (lane < y * seg + 6)
         mine = (lane >= y * seg) & (lane < (y + 1) * seg)
         for c in range(fields):
             w_ref[y, c] = w[c]
@@ -120,8 +128,16 @@
                 down_ref[y * fields + c] = w[c]
             low = pltpu.roll(w[c], (y * seg + 3) % nx, 1)
             high = pltpu.roll(w[c], (y * seg + 10) % nx, 1)
-            edge_ref[c] = jnp.where(mine, jnp.where(first, low, high), edge_ref[c])
-        b = primitive([base_ref[c, :, y, :] for c in range(fields)])
+            both = jnp.where(first, low, high)
+            edge_ref[c] = both if y == 0 else jnp.where(mine, both, edge_ref[c])
+    for load in loads[fields:]:
+        load.wait()
+    fastest = None
+    for y in range(ny):
+        b = [base_ref[c, :, y, :] for c in range(fields)]
+        for c in range(fields):
+            old_ref[y, c] = b[c] * (1.0 / 3.0) + (2.0 / 3.0) * now_ref[c, :, y, :]
+        b = primitive(b)
         stiff_gamma, stiff_term = mixture(b[6])
         speed = jnp.maximum(jnp.maximum(jnp.abs(b[2]), jnp.abs(b[3])), jnp.abs(b[4]))
         speed = speed + sound(b, b[0] + b[1], stiff_gamma, stiff_term)
@@ -216,16 +232,16 @@
 
 
 def stream_kernel(
-    place_ref, w_ref, edge_ref, left_ref, right_ref, in_ref, acc_ref, rate_ref,
-    ring, sides, seam, flux_ref, keep,
+    w_ref, edge_ref, left_ref, right_ref, in_ref, acc_ref, rate_ref, ring, flux_ref, keep
 ):
     ny, _, nz, nx = w_ref.shape
     seg = nx // ny
     lane = lane_of((nz, nx))
     part = lane % seg
-    is_first = place_ref[0] == 1
-    is_last = place_ref[1] == 1
-
+    is_first = left_ref[fields] <= 0.0
+    is_last = right_ref[fields] <= 0.0
+
+    left, right = [], []
     for k in range(fields):
         e = edge_ref[k]
         last = jnp.where(
@@ -234,31 +250,29 @@
         lower = jnp.where(is_first, in_ref[k], left_ref[k])
         upper = jnp.where(is_last, last, right_ref[k])
         e = jnp.where(part < 3, lower, jnp.where((part >= 10) & (part < 13), upper, e))
+        ring[k] = jnp.where(part < 3, e, pltpu.roll(e, nx - 7, 1))
         c = pltpu.roll(e, nx - 1, 1) - e
-        ring[k] = c
         up, down = cell_faces(
             k, pltpu.roll(c, 2, 1), pltpu.roll(c, 1, 1), c, pltpu.roll(c, nx - 1, 1), e
         )
-        sides[k] = up
-        sides[fields + k] = down
+        left.append(pltpu.roll(up, 1, 1))
+        right.append(down)
+    outer = face_flux(left, right, 0)
+    for k in range(fields + 1):
+        keep[k] = jnp.where(part == 2, pltpu.roll(outer[k], nx - 8, 1), outer[k])
 
     def stream(y, _):
         base = y * seg
         left, right = [], []
-        at_seam = lane == base + 10
         for k in range(fields):
             h = w_ref[y, k]
-            de = ring[k]
-            tail = pltpu.roll(de, nx - 11 - base, 1)
-            head = pltpu.roll(de, nx - 1 - base, 1)
-            c = jnp.where(lane == nx - 1, pltpu.roll(tail, 1, 1), pltpu.roll(h, nx - 1, 1) - h)
-            d = jnp.where(lane == nx - 1, tail, pltpu.roll(c, nx - 1, 1))
-            a = jnp.where(lane < 2, head, pltpu.roll(c, 2, 1))
-            b = jnp.where(lane < 1, pltpu.roll(head, nx - 1, 1), pltpu.roll(c, 1, 1))
-            up, down = cell_faces(k, a, b, c, d, h)
-            seam[k] = jnp.where(at_seam, pltpu.roll(up, base + 11, 1), seam[k])
-            edge_up = pltpu.roll(sides[k], nx - base - 2, 1)
-            left.append(jnp.where(lane < 1, edge_up, pltpu.roll(up, 1, 1)))
+            beyond = pltpu.roll(ring[k], nx - 3 - base, 1)
+            f = pltpu.roll(jnp.where(lane >= nx - 2, beyond, h), 2, 1)
+            g = pltpu.roll(jnp.where(lane == nx - 1, beyond, h), 1, 1)
+            kk = pltpu.roll(jnp.where(lane == 0, beyond, h), nx - 1, 1)
+            l = pltpu.roll(jnp.where(lane < 2, beyond, h), nx - 2, 1)
+            up, down = cell_faces(k, g - f, h - g, kk - h, l - kk, h)
+            left.append(pltpu.roll(up, 1, 1))
             right.append(down)
         flux = face_flux(left, right, 0)
         for k in range(fields + 1):
@@ -266,18 +280,14 @@
         return 0
 
     lax.fori_loop(0, ny, stream, 0)
-    outer = face_flux(
-        [seam[k] for k in range(fields)], [sides[fields + k] for k in range(fields)], 0
-    )
-    for k in range(fields + 1):
-        keep[k] = outer[k]
-
     for y in range(ny):
         diff = []
         for k in range(fields + 1):
             f = flux_ref[y, k]
-            end = pltpu.roll(keep[k], (2 * nx - 1 - 10 - y * seg) % nx, 1)
-            diff.append(jnp.where(lane == nx - 1, end, pltpu.roll(f, nx - 1, 1)) - f)
+            ends = pltpu.roll(keep[k], (nx - 3 - y * seg) % nx, 1)
+            here = jnp.where(lane == 0, ends, f)
+            after = jnp.where(lane == nx - 1, ends, pltpu.roll(f, nx - 1, 1))
+            diff.append(after - here)
         for k in range(fields):
             rate = acc_ref[y, k] - diff[k]
             if k == 6:
@@ -285,14 +295,18 @@
             rate_ref[y, k] = rate
 
 
-def update_kernel(rate_ref, mine_ref, peer_ref, now_ref, base_ref, out_ref):
+def update_kernel(rate_ref, mine_ref, peer_ref, old_ref, out_hbm, out_ref, sems):
     ny, _, nz, nx = rate_ref.shape
     fastest = jnp.max(jnp.maximum(mine_ref[...], peer_ref[...]))
     step = (2.0 / 3.0) * (courant / jnp.full((nz, nx), fastest, jnp.float32))
-    for y in range(ny):
-        for k in range(fields):
-            old = base_ref[k, :, y, :] * (1.0 / 3.0) + (2.0 / 3.0) * now_ref[k, :, y, :]
-            out_ref[k, :, y, :] = old + step * rate_ref[y, k]
+    stores = []
+    for k in range(fields):
+        for y in range(ny):
+            out_ref[k, :, y, :] = old_ref[y, k] + step * rate_ref[y, k]
+        stores.append(pltpu.make_async_copy(out_ref.at[k], out_hbm.at[k], sems.at[k]))
+        stores[-1].start()
+    for store in stores:
+        store.wait()
 
 
 def buffer(*shape):
@@ -318,20 +332,32 @@
     width = ghost * fields + 1
     wide = buffer(ny, fields, nz, nx)
     vmem = pl.BlockSpec(memory_space=pltpu.VMEM)
-    state_now, state_base = near(state_now, state_base)
-    w, up, down, edge = pl.pallas_call(
+    whole = pl.BlockSpec(memory_space=pl.ANY)
+    w, up, down, edge, old = pl.pallas_call(
         pack_kernel,
-        out_shape=(wide, buffer(width, nz, nx), buffer(width, nz, nx), buffer(fields + 1, nz, nx)),
-        in_specs=[vmem] * 2,
-        out_specs=(vmem,) * 4,
+        out_shape=(
+            wide,
+            buffer(width, nz, nx),
+            buffer(width, nz, nx),
+            buffer(fields + 1, nz, nx),
+            wide,
+        ),
+        in_specs=[whole] * 2,
+        out_specs=(vmem,) * 5,
+        scratch_shapes=[
+            buffer(fields, nz, ny, nx),
+            buffer(fields, nz, ny, nx),
+            pltpu.SemaphoreType.DMA((2 * fields,)),
+        ],
         name="pack",
     )(state_now, state_base)
 
     streams, crosses = lax.axis_size("stream"), lax.axis_size("cross")
     low = lax.ppermute(up, "cross", ring_pairs(crosses, 1))
     high = lax.ppermute(down, "cross", ring_pairs(crosses, -1))
-    left = lax.ppermute(edge, "stream", ring_pairs(streams, 1))
-    right = lax.ppermute(edge, "stream", ring_pairs(streams, -1))
+    onward = [(i, i + 1) for i in range(streams - 1)]
+    left = lax.ppermute(edge, "stream", onward)
+    right = lax.ppermute(edge, "stream", [(j, i) for i, j in onward])
 
     rate, inner = pl.pallas_call(
         span_kernel,
@@ -340,9 +366,6 @@
         out_specs=(vmem,) * 2,
         name="span",
     )(*near(w, jnp.transpose(inflow, (0, 3, 1, 2))))
-
-    position = lax.axis_index("stream")
-    place = jnp.stack([position == 0, position == streams - 1]).astype(jnp.int32)
 
     def cross_sweep():
         return pl.pallas_call(
@@ -361,17 +384,15 @@
         return pl.pallas_call(
             stream_kernel,
             out_shape=wide,
-            in_specs=[pl.BlockSpec(memory_space=pltpu.SMEM)] + [vmem] * 6,
+            in_specs=[vmem] * 6,
             out_specs=vmem,
             scratch_shapes=[
-                buffer(fields, nz, nx),
-                buffer(2 * fields, nz, nx),
                 buffer(fields, nz, nx),
                 buffer(ny, fields + 1, nz, nx),
                 buffer(fields + 1, nz, nx),
             ],
             name="stream",
-        )(place, *near(w, edge, left, right, inner, acc))
+        )(*near(w, edge, left, right, inner, acc))
 
     speed = jnp.maximum(jnp.maximum(low[-1], high[-1]), edge[-1])
     speed, rate = lax.optimization_barrier((speed, rate))
@@ -393,10 +414,14 @@
     return pl.pallas_call(
         update_kernel,
         out_shape=jax.ShapeDtypeStruct(state_now.shape, jnp.float32),
-        in_specs=[vmem] * 5,
-        out_specs=vmem,
+        in_specs=[vmem] * 4,
+        out_specs=whole,
+        scratch_shapes=[
+            buffer(fields, nz, ny, nx),
+            pltpu.SemaphoreType.DMA((fields,)),
+        ],
         name="update",
-    )(*near(rate, speed, peer, state_now, state_base))
+    )(*near(rate, speed, peer, old))
 
 
 def solution(mesh):

time: 29.4 us -> 28.6 us (0.973)
  starting transfers between devices: 13.3 us -> 17.2 us
  waiting for transfers between devices: 4.3 us -> 2.12 us
  local copies, waits for them, and re-layouts: 1.88 us -> 0.01 us
  other arithmetic: 0.63 us -> 0.01 us
    ppermute x1, starting transfers between devices: 0.01 us -> 2.92 us  [shards(): speed = jnp.maximum(speed, lax.ppermute(speed, 'stream', pairs))]
    unnamed x8 -> x2, local copies, waits for them, and re-layouts: 1.88 us -> 0.01 us
    ppermute x1, waiting for transfers between devices: 1.58 us -> 0.01 us  [shards(): ahead = lax.ppermute(speed, 'cross', ring_pairs(crosses, reach))]
    pallas_call x1, Pallas kernels: 0.78 us -> 2.21 us  [shards(): pl.pallas_call(pack_kernel, out_shape=(wide, buffer(width, nz, nx), buffe...]
    pallas_call x1, Pallas kernels: 4.39 us -> 3.2 us  [stream_sweep(): pl.pallas_call(stream_kernel, out_shape=wide, in_specs=[vmem] * 6, out_sp...]
    ppermute x2, starting transfers between devices: 1.75 us -> 2.57 us  [the longest x1 1.29 us: shards(): right = lax.ppermute(edge, 'stream', [(j, i) for i, j in onward])]
    convert_element_type x1 -> x0, other arithmetic: 0.62 us -> none  [shards(): jnp.stack([position == 0, position == streams - 1]).astype(jnp.int32)]
    ppermute x1, waiting for transfers between devices: 0.6 us -> 0.01 us  [shards(): behind = lax.ppermute(speed, 'cross', ring_pairs(crosses, -reach))]
  transfers between devices with their start and end apart: 8 -> 8, of which waited for: 4 -> 2; matrix products, arithmetic and copies ran while one was open for 2% -> 0% of each run, Pallas kernels for 24% -> 21%
where the time goes in v3:
time: 28.6 us; the launch traced here: 28.4 us
  starting transfers between devices  17.2 us (60%)
  Pallas kernels  9.04 us (32%)
  waiting for transfers between devices  2.12 us (7%)
    pallas_call x1, Pallas kernels, stream_sweep(): pl.pallas_call(stream_kernel, out_shape=wide, in_specs=[vmem] * 6, out_sp...  3.2 us
    ppermute x1, starting transfers between devices, shards(): high = lax.ppermute(down, 'cross', ring_pairs(crosses, -1))  3.1 us
    ppermute x1, starting transfers between devices, shards(): low = lax.ppermute(up, 'cross', ring_pairs(crosses, 1))  3.05 us
    ppermute x1, starting transfers between devices, shards(): speed = jnp.maximum(speed, lax.ppermute(speed, 'stream', pairs))  2.92 us
    ppermute x1, starting transfers between devices, shards(): behind = lax.ppermute(speed, 'cross', ring_pairs(crosses, -reach))  2.32 us
    pallas_call x1, Pallas kernels, shards(): pl.pallas_call(pack_kernel, out_shape=(wide, buffer(width, nz, nx), buffe...  2.21 us
    ppermute x1, starting transfers between devices, shards(): peer = lax.ppermute(speed, 'stream', hop_pairs(streams, hop, streams - hop))  1.7 us
    ppermute x1, starting transfers between devices, shards(): ahead = lax.ppermute(speed, 'cross', ring_pairs(crosses, reach))  1.5 us
  transfers between devices with their start and end apart: 8, of which 2 were waited for; matrix products, arithmetic and copies ran while one was open for 0% of the time, Pallas kernels for 21%

profile of v3, /device:TPU:0, one launch (start us, length us, event | category | flops | bytes accessed | tf_op | source)
XLA Modules:
  0.0 28.4 jit_solution(15214316874652942421)
XLA Ops:
  0.0 0.0 copy-start
  0.0 2.2 %pack.1 = (f32[8,7,8,128]{3,2,1,0:T(8,128)S(1)}, f32[22,8,128]{2,1,0:T(8,128)S(1)}, f32[22,8,128]{2,1,0:T(8,128)S(1)}, f32[8,8,128]{2,1,0:T(8,128)S(1)}, f32[8,7,8,128]{3,2,1,0:T(8,128)S(1)}) custom-call(f32[7,8,8,128]{3,2,1,0:T(8,128)} %now_hbm.1, f32[7,8,8,128]{3,2,1,0:T(8,128)} %base_hbm.1), custom_call_target="tpu_custom_call" | custom-call | tf_op jit(solution)/shard_map/pack/pallas_call | solution.py:336
  2.2 3.0 %collective-permute-start.2 = (f32[22,8,128]{2,1,0:T(8,128)S(1)}, f32[22,8,128]{2,1,0:T(8,128)S(1)}, u32[]{:S(2)}, u32[]{:S(2)}) collective-permute-start(f32[22,8,128]{2,1,0:T(8,128)S(1)} %get-tuple-element.19), channel_id=1, source_target_pairs={{0,1},{1,2},{2,3},{3,4},{4,5},{5,6},{6,7},{7,0},{8,9},{9,10},{10,1... | collective-permute-start | bytes 270344 | tf_op jit(solution)/shard_map/ppermute | solution.py:356
  5.3 3.1 %collective-permute-start.3 = (f32[22,8,128]{2,1,0:T(8,128)S(1)}, f32[22,8,128]{2,1,0:T(8,128)S(1)}, u32[]{:S(2)}, u32[]{:S(2)}) collective-permute-start(f32[22,8,128]{2,1,0:T(8,128)S(1)} %get-tuple-element.20), channel_id=1, source_target_pairs={{0,7},{1,0},{2,1},{3,2},{4,3},{5,4},{6,5},{7,6},{8,15},{9,8},{10,9... | collective-permute-start | bytes 270344 | tf_op jit(solution)/shard_map/ppermute | solution.py:357
  8.4 0.0 copy-done
  8.4 1.2 %span.1 = (f32[8,7,8,128]{3,2,1,0:T(8,128)S(1)}, f32[7,8,128]{2,1,0:T(8,128)S(1)}) custom-call(f32[8,7,8,128]{3,2,1,0:T(8,128)S(1)} %get-tuple-element.16.w_ref, f32[7,3,8,8]{3,2,1,0:T(8,128)S(1)} %bitcast.3), custom_call_target="tpu_custom_call" | custom-call | tf_op jit(solution)/shard_map/span/pallas_call | solution.py:362
  9.6 1.4 %collective-permute-done.2.low_ref = f32[22,8,128]{2,1,0:T(8,128)S(1)} collective-permute-done((f32[22,8,128]{2,1,0:T(8,128)S(1)}, f32[22,8,128]{2,1,0:T(8,128)S(1)}, u32[]{:S(2)}, u32[]{:S(2)}) %collective-permute-start.2) | collective-permute-done | bytes 90144 | tf_op jit(solution)/shard_map/ppermute | solution.py:356
  11.0 0.7 %collective-permute-done.3.high_ref = f32[22,8,128]{2,1,0:T(8,128)S(1)} collective-permute-done((f32[22,8,128]{2,1,0:T(8,128)S(1)}, f32[22,8,128]{2,1,0:T(8,128)S(1)}, u32[]{:S(2)}, u32[]{:S(2)}) %collective-permute-start.3) | collective-permute-done | bytes 90144 | tf_op jit(solution)/shard_map/ppermute | solution.py:357
  11.7 1.5 %collective-permute-start.4 = (f32[8,128]{1,0:T(8,128)S(1)}, f32[8,128]{1,0:T(8,128)S(1)}, u32[]{:S(2)}, u32[]{:S(2)}) collective-permute-start(f32[8,128]{1,0:T(8,128)S(1)} %fusion.1), channel_id=1, source_target_pairs={{0,3},{1,4},{2,5},{3,6},{4,7},{5,0},{6,1},{7,2},{8,11},{9,12},{10,... | collective-permute-start | bytes 12296 | tf_op jit(solution)/shard_map/ppermute | solution.py:401
  13.2 2.3 %collective-permute-start.5 = (f32[8,128]{1,0:T(8,128)S(1)}, f32[8,128]{1,0:T(8,128)S(1)}, u32[]{:S(2)}, u32[]{:S(2)}) collective-permute-start(f32[8,128]{1,0:T(8,128)S(1)} %fusion.1), channel_id=1, source_target_pairs={{0,5},{1,6},{2,7},{3,0},{4,1},{5,2},{6,3},{7,4},{8,13},{9,14},{10,... | collective-permute-start | bytes 12296 | tf_op jit(solution)/shard_map/ppermute | solution.py:402
  15.6 1.3 %collective-permute-start = (f32[8,8,128]{2,1,0:T(8,128)S(1)}, f32[8,8,128]{2,1,0:T(8,128)S(1)}, u32[]{:S(2)}, u32[]{:S(2)}) collective-permute-start(f32[8,8,128]{2,1,0:T(8,128)S(1)} %get-tuple-element.17.edge_ref), channel_id=1, source_target_pairs={{0,8},{8,16},{16,24},{1,9},{9,17},{17,25},{2,10},{10,18},{18,26},{... | collective-permute-start | bytes 98312 | tf_op jit(solution)/shard_map/ppermute | solution.py:359
  16.8 1.3 %collective-permute-start.1 = (f32[8,8,128]{2,1,0:T(8,128)S(1)}, f32[8,8,128]{2,1,0:T(8,128)S(1)}, u32[]{:S(2)}, u32[]{:S(2)}) collective-permute-start(f32[8,8,128]{2,1,0:T(8,128)S(1)} %get-tuple-element.17.edge_ref), channel_id=1, source_target_pairs={{8,0},{16,8},{24,16},{9,1},{17,9},{25,17},{10,2},{18,10},{26,18},{... | collective-permute-start | bytes 98312 | tf_op jit(solution)/shard_map/ppermute | solution.py:360
  18.1 0.0 collective-permute-done.4
  18.2 0.0 collective-permute-done.5
  18.2 2.9 %collective-permute-start.6 = (f32[8,128]{1,0:T(8,128)S(1)}, f32[8,128]{1,0:T(8,128)S(1)}, u32[]{:S(2)}, u32[]{:S(2)}) collective-permute-start(f32[8,128]{1,0:T(8,128)S(1)} %maximum_maximum_fusion), channel_id=1, source_target_pairs={{0,8},{8,0},{16,24},{24,16},{1,9},{9,1},{17,25},{25,17},{2,10},{10... | collective-permute-start | bytes 12296 | tf_op jit(solution)/shard_map/ppermute | solution.py:409
  21.1 1.4 %cross.1.acc_ref = f32[8,7,8,128]{3,2,1,0:T(8,128)S(1)} custom-call(f32[8,7,8,128]{3,2,1,0:T(8,128)S(1)} %get-tuple-element.16.w_ref, f32[8,7,8,128]{3,2,1,0:T(8,128)S(1)} %get-tuple-element.23.rate_ref, f32[22,8,128]{2,1,0:T(8,128)S(1)} %collective-permute-done.2.low_ref, f32[22,8,128]{2,1,0:T(8,128)S(1)} %collective-permute-done.3.high_ref), custom_call_target="tpu_custom_call" | custom-call | tf_op jit(solution)/shard_map/cross/pallas_call | solution.py:371
  22.5 0.0 collective-permute-done.6
  22.6 1.7 %collective-permute-start.7 = (f32[8,128]{1,0:T(8,128)S(1)}, f32[8,128]{1,0:T(8,128)S(1)}, u32[]{:S(2)}, u32[]{:S(2)}) collective-permute-start(f32[8,128]{1,0:T(8,128)S(1)} %max.24.mine_ref), channel_id=1, source_target_pairs={{0,16},{8,24},{16,0},{24,8},{1,17},{9,25},{17,1},{25,9},{2,18},{10... | collective-permute-start | bytes 12296 | tf_op jit(solution)/shard_map/ppermute | solution.py:412
  24.3 0.0 collective-permute-done.left_ref
  24.3 0.0 collective-permute-done.1.right_ref
  24.3 3.2 %stream.1.rate_ref = f32[8,7,8,128]{3,2,1,0:T(8,128)S(1)} custom-call(f32[8,7,8,128]{3,2,1,0:T(8,128)S(1)} %get-tuple-element.16.w_ref, f32[8,8,128]{2,1,0:T(8,128)S(1)} %get-tuple-element.17.edge_ref, f32[8,8,128]{2,1,0:T(8,128)S(1)} %collective-permute-done.left_ref, f32[8,8,128]{2,1,0:T(8,128)S(1)} %collective-permute-done.1.right_ref, ...), custom_call_target="tpu_custom_call" | custom-call | tf_op jit(solution)/shard_map/stream/pallas_call | solution.py:384
  27.5 0.0 collective-permute-done.7.peer_ref
  27.5 0.9 %update.1 = f32[7,8,8,128]{3,2,1,0:T(8,128)} custom-call(f32[8,7,8,128]{3,2,1,0:T(8,128)S(1)} %stream.1.rate_ref, f32[8,128]{1,0:T(8,128)S(1)} %max.24.mine_ref, f32[8,128]{1,0:T(8,128)S(1)} %collective-permute-done.7.peer_ref, f32[8,7,8,128]{3,2,1,0:T(8,128)S(1)} %get-tuple-element.26.old_ref), custom_call_target="tpu_custom_call" | custom-call | tf_op jit(solution)/shard_map/update/pallas_call | solution.py:414
  (3 shorter events, 0.0 us)
Async XLA Ops:
  0.0 8.4 %copy-start = (f32[7,8,8,3]{2,1,3,0:T(8,128)S(1)}, f32[7,8,8,3]{2,1,3,0:T(8,128)}, u32[]{:S(2)}) copy-start(f32[7,8,8,3]{2,1,3,0:T(8,128)} %param.5) | copy-start | bytes 16132
  2.2 8.8 %collective-permute-start.2 = (f32[22,8,128]{2,1,0:T(8,128)S(1)}, f32[22,8,128]{2,1,0:T(8,128)S(1)}, u32[]{:S(2)}, u32[]{:S(2)}) collective-permute-start(f32[22,8,128]{2,1,0:T(8,128)S(1)} %get-tuple-element.19), channel_id=1, source_target_pairs={{0,1},{1,2},{2,3},{3,4},{4,5},{5,6},{6,7},{7,0},{8,9},{9,10},{10,1... | collective-permute-start | bytes 270344 | tf_op jit(solution)/shard_map/ppermute | solution.py:356
  5.3 6.5 %collective-permute-start.3 = (f32[22,8,128]{2,1,0:T(8,128)S(1)}, f32[22,8,128]{2,1,0:T(8,128)S(1)}, u32[]{:S(2)}, u32[]{:S(2)}) collective-permute-start(f32[22,8,128]{2,1,0:T(8,128)S(1)} %get-tuple-element.20), channel_id=1, source_target_pairs={{0,7},{1,0},{2,1},{3,2},{4,3},{5,4},{6,5},{7,6},{8,15},{9,8},{10,9... | collective-permute-start | bytes 270344 | tf_op jit(solution)/shard_map/ppermute | solution.py:357
  11.7 6.4 %collective-permute-start.4 = (f32[8,128]{1,0:T(8,128)S(1)}, f32[8,128]{1,0:T(8,128)S(1)}, u32[]{:S(2)}, u32[]{:S(2)}) collective-permute-start(f32[8,128]{1,0:T(8,128)S(1)} %fusion.1), channel_id=1, source_target_pairs={{0,3},{1,4},{2,5},{3,6},{4,7},{5,0},{6,1},{7,2},{8,11},{9,12},{10,... | collective-permute-start | bytes 12296 | tf_op jit(solution)/shard_map/ppermute | solution.py:401
  13.2 4.9 %collective-permute-start.5 = (f32[8,128]{1,0:T(8,128)S(1)}, f32[8,128]{1,0:T(8,128)S(1)}, u32[]{:S(2)}, u32[]{:S(2)}) collective-permute-start(f32[8,128]{1,0:T(8,128)S(1)} %fusion.1), channel_id=1, source_target_pairs={{0,5},{1,6},{2,7},{3,0},{4,1},{5,2},{6,3},{7,4},{8,13},{9,14},{10,... | collective-permute-start | bytes 12296 | tf_op jit(solution)/shard_map/ppermute | solution.py:402
  15.6 8.7 %collective-permute-start = (f32[8,8,128]{2,1,0:T(8,128)S(1)}, f32[8,8,128]{2,1,0:T(8,128)S(1)}, u32[]{:S(2)}, u32[]{:S(2)}) collective-permute-start(f32[8,8,128]{2,1,0:T(8,128)S(1)} %get-tuple-element.17.edge_ref), channel_id=1, source_target_pairs={{0,8},{8,16},{16,24},{1,9},{9,17},{17,25},{2,10},{10,18},{18,26},{... | collective-permute-start | bytes 98312 | tf_op jit(solution)/shard_map/ppermute | solution.py:359
  16.8 7.4 %collective-permute-start.1 = (f32[8,8,128]{2,1,0:T(8,128)S(1)}, f32[8,8,128]{2,1,0:T(8,128)S(1)}, u32[]{:S(2)}, u32[]{:S(2)}) collective-permute-start(f32[8,8,128]{2,1,0:T(8,128)S(1)} %get-tuple-element.17.edge_ref), channel_id=1, source_target_pairs={{8,0},{16,8},{24,16},{9,1},{17,9},{25,17},{10,2},{18,10},{26,18},{... | collective-permute-start | bytes 98312 | tf_op jit(solution)/shard_map/ppermute | solution.py:360
  18.2 4.4 %collective-permute-start.6 = (f32[8,128]{1,0:T(8,128)S(1)}, f32[8,128]{1,0:T(8,128)S(1)}, u32[]{:S(2)}, u32[]{:S(2)}) collective-permute-start(f32[8,128]{1,0:T(8,128)S(1)} %maximum_maximum_fusion), channel_id=1, source_target_pairs={{0,8},{8,0},{16,24},{24,16},{1,9},{9,1},{17,25},{25,17},{2,10},{10... | collective-permute-start | bytes 12296 | tf_op jit(solution)/shard_map/ppermute | solution.py:409
  22.6 4.9 %collective-permute-start.7 = (f32[8,128]{1,0:T(8,128)S(1)}, f32[8,128]{1,0:T(8,128)S(1)}, u32[]{:S(2)}, u32[]{:S(2)}) collective-permute-start(f32[8,128]{1,0:T(8,128)S(1)} %max.24.mine_ref), channel_id=1, source_target_pairs={{0,16},{8,24},{16,0},{24,8},{1,17},{9,25},{17,1},{25,9},{2,18},{10... | collective-permute-start | bytes 12296 | tf_op jit(solution)/shard_map/ppermute | solution.py:412
